TPU v7x, 32 devices: a whole 2x2x4 slice. The times are simulated.
32 devices in a mesh: ctx: 16 (over z, y, core), fsdp: 2 (over x).
Axes of the slice: x: 2, y: 2, z: 4, core: 2. Of those that a mesh axis runs over, the one named last changes fastest.
Arguments:
- tokens: bfloat16 [2, 4096, 768], P('fsdp', 'ctx'), may hold values from -6 to 6
- lengths: int32 [2], P('fsdp'), may hold values from 1024 to 4096, as said below
- cotangent: bfloat16 [2, 4096, 768], P('fsdp', 'ctx'), may hold values from -6 to 6
- query_weight: bfloat16 [768, 768], P('ctx', 'fsdp'), may hold values from -0.21875 to 0.21875
- key_weight: bfloat16 [768, 768], P('ctx', 'fsdp'), may hold values from -0.21875 to 0.21875
- value_weight: bfloat16 [768, 768], P('ctx', 'fsdp'), may hold values from -0.21875 to 0.21875
- out_weight: bfloat16 [768, 768], P('ctx', 'fsdp'), may hold values from -6 to 6
- in_weight: bfloat16 [768, 3072], P('ctx', 'fsdp'), may hold values from -0.21875 to 0.21875
- down_weight: bfloat16 [3072, 768], P('ctx', 'fsdp'), may hold values from -0.109375 to 0.109375
- query_bias: bfloat16 [768], P('ctx'), may hold values from -3 to 3
- value_bias: bfloat16 [768], P('ctx'), may hold values from -0.119628906 to 0.119628906
- out_bias: bfloat16 [768], P('ctx'), may hold values from -3 to 3
- attn_norm_gain: bfloat16 [768], P('ctx'), may hold values from 0.5 to 1.5
- attn_norm_bias: bfloat16 [768], P('ctx'), may hold values from -2 to 2
- in_bias: bfloat16 [3072], P('ctx'), may hold values from -3 to 3
- down_bias: bfloat16 [768], P('ctx'), may hold values from -3 to 3
- ffn_norm_gain: bfloat16 [768], P('ctx'), may hold values from 0.5 to 1.5
- ffn_norm_bias: bfloat16 [768], P('ctx'), may hold values from -2 to 2
Outputs:
- layer_out: bfloat16 [2, 4096, 768], P('fsdp', 'ctx')
- tokens_grad: bfloat16 [2, 4096, 768], P('fsdp', 'ctx')
- grad_query_weight: float32 [768, 768], P('ctx', 'fsdp')
- grad_key_weight: float32 [768, 768], P('ctx', 'fsdp')
- grad_value_weight: float32 [768, 768], P('ctx', 'fsdp')
- grad_out_weight: float32 [768, 768], P('ctx', 'fsdp')
- grad_in_weight: float32 [768, 3072], P('ctx', 'fsdp')
- grad_down_weight: float32 [3072, 768], P('ctx', 'fsdp')
- grad_query_bias: float32 [768], P('ctx')
- grad_value_bias: float32 [768], P('ctx')
- grad_out_bias: float32 [768], P('ctx')
- grad_attn_norm_gain: float32 [768], P('ctx')
- grad_attn_norm_bias: float32 [768], P('ctx')
- grad_in_bias: float32 [3072], P('ctx')
- grad_down_bias: float32 [768], P('ctx')
- grad_ffn_norm_gain: float32 [768], P('ctx')
- grad_ffn_norm_bias: float32 [768], P('ctx')
- rms_values: float32 [3], replicated
Inputs may be any that keep to these rules, and one draw needn't show every extreme that they name: `lengths`: each sequence has between 1024 and 4096 valid slots; some sequence has exactly 4096, another exactly 1024.
All inputs are finite; a program needn't handle non-finite values.
Results may differ from a plain program's by a relative error of at most 0.022.
Values may be sent and summed in bfloat16 or wider, within the bound.
No kernel may reach another device: no remote copies, remote signals or barrier semaphores. Data moves between devices by JAX's collectives and lax.ppermute only.
A program may use at most 192 MiB of HBM per device.

v0:
```python
import functools

import jax
import jax.numpy as jnp
from jax import lax
from jax.experimental import pallas as pl
from jax.experimental.pallas import tpu as pltpu
from jax.sharding import PartitionSpec as P

HEAD_DIM = 64


norm_eps = 1e-12
score_scale = 0.125
masked_score = -1000000000.0
rows_contract = (((0,), (0,)), ((), ()))
columns_contract = (((1,), (1,)), ((), ()))


def layer_norm(stream, gain_vec, shift_vec):
    center = jnp.mean(stream, axis=-1, keepdims=True)
    offset = stream - center
    spread = jnp.mean(offset * offset, axis=-1, keepdims=True)
    return offset * lax.rsqrt(spread + norm_eps) * gain_vec + shift_vec


def gelu_exact(inner_pre):
    return jax.nn.gelu(inner_pre, approximate=False)


def plain_product(left_side, right_side):
    return jnp.dot(left_side, right_side, preferred_element_type=jnp.float32)


def row_product(left_side, right_side):
    return lax.dot_general(left_side, right_side, rows_contract, preferred_element_type=jnp.float32)


def column_product(left_side, right_side):
    return lax.dot_general(
        left_side, right_side, columns_contract, preferred_element_type=jnp.float32
    )


def head_scores(query_head, key_head, key_ok):
    scores = (
        jnp.einsum("sqd,skd->sqk", query_head, key_head, preferred_element_type=jnp.float32)
        * score_scale
    )
    return jnp.where(key_ok[:, None, :], scores, masked_score)


def attend(query_seq, pair_all, key_ok):
    seq_count, slot_count, model_width = query_seq.shape
    heads_count = model_width // HEAD_DIM

    def one_head(head_index, loop_state):
        mixed_out, log_totals = loop_state
        head_start = head_index * HEAD_DIM
        query_head = lax.dynamic_slice_in_dim(query_seq, head_start, HEAD_DIM, 2)
        key_head = lax.dynamic_slice_in_dim(pair_all, head_start, HEAD_DIM, 2)
        value_head = lax.dynamic_slice_in_dim(pair_all, model_width + head_start, HEAD_DIM, 2)
        scores = head_scores(query_head, key_head, key_ok)
        row_peak = jnp.max(scores, axis=-1, keepdims=True)
        row_expo = jnp.exp(scores - row_peak)
        row_total = jnp.sum(row_expo, axis=-1, keepdims=True)
        attn_probs = (row_expo / row_total).astype(jnp.bfloat16)
        head_out = jnp.einsum(
            "sqk,skd->sqd", attn_probs, value_head, preferred_element_type=jnp.float32
        )
        mixed_out = lax.dynamic_update_slice_in_dim(mixed_out, head_out, head_start, 2)
        log_row = row_peak[..., 0] + jnp.log(row_total[..., 0])
        log_totals = lax.dynamic_update_index_in_dim(log_totals, log_row, head_index, 0)
        return (mixed_out, log_totals)

    start_state = (
        jnp.zeros((seq_count, slot_count, model_width), jnp.float32),
        jnp.zeros((heads_count, seq_count, slot_count), jnp.float32),
    )
    return lax.fori_loop(0, heads_count, one_head, start_state)


def attend_back(query_seq, pair_all, key_ok, log_totals, grad_mixed):
    seq_count, slot_count, model_width = query_seq.shape
    heads_count = model_width // HEAD_DIM

    def one_head(head_index, loop_state):
        grad_query, grad_pair = loop_state
        head_start = head_index * HEAD_DIM
        query_head = lax.dynamic_slice_in_dim(query_seq, head_start, HEAD_DIM, 2)
        key_head = lax.dynamic_slice_in_dim(pair_all, head_start, HEAD_DIM, 2)
        value_head = lax.dynamic_slice_in_dim(pair_all, model_width + head_start, HEAD_DIM, 2)
        grad_head = lax.dynamic_slice_in_dim(grad_mixed, head_start, HEAD_DIM, 2)
        scores = head_scores(query_head, key_head, key_ok)
        log_row = lax.dynamic_index_in_dim(log_totals, head_index, 0, keepdims=False)
        attn_probs = jnp.exp(scores - log_row[..., None])
        probs_b = attn_probs.astype(jnp.bfloat16)
        grad_probs = jnp.einsum(
            "sqd,skd->sqk", grad_head, value_head, preferred_element_type=jnp.float32
        )
        row_inner = jnp.sum(attn_probs * grad_probs, axis=-1, keepdims=True)
        grad_scores = (attn_probs * (grad_probs - row_inner)).astype(jnp.bfloat16)
        grad_query_head = (
            jnp.einsum("sqk,skd->sqd", grad_scores, key_head, preferred_element_type=jnp.float32)
            * score_scale
        )
        grad_key_head = (
            jnp.einsum("sqk,sqd->skd", grad_scores, query_head, preferred_element_type=jnp.float32)
            * score_scale
        )
        grad_value_head = jnp.einsum(
            "sqk,sqd->skd", probs_b, grad_head, preferred_element_type=jnp.float32
        )
        grad_query = lax.dynamic_update_slice_in_dim(grad_query, grad_query_head, head_start, 2)
        grad_pair = lax.dynamic_update_slice_in_dim(grad_pair, grad_key_head, head_start, 2)
        grad_pair = lax.dynamic_update_slice_in_dim(
            grad_pair, grad_value_head, model_width + head_start, 2
        )
        return (grad_query, grad_pair)

    start_state = (jnp.zeros(query_seq.shape, jnp.float32), jnp.zeros(pair_all.shape, jnp.float32))
    return lax.fori_loop(0, heads_count, one_head, start_state)


def column_sums(matrix_b):
    return jnp.sum(matrix_b.astype(jnp.float32), axis=0)


def body(
    tokens,
    lengths,
    cotangent,
    query_weight,
    key_weight,
    value_weight,
    out_weight,
    in_weight,
    down_weight,
    query_bias,
    value_bias,
    out_bias,
    attn_norm_gain,
    attn_norm_bias,
    in_bias,
    down_bias,
    ffn_norm_gain,
    ffn_norm_bias,
):
    seq_count, slot_count, model_width = tokens.shape
    row_count = seq_count * slot_count
    ctx_size = lax.axis_size("ctx")
    ctx_index = lax.axis_index("ctx")
    row_parts = (
        lax.all_gather(query_weight, "ctx", axis=0, tiled=True),
        lax.all_gather(key_weight, "ctx", axis=0, tiled=True),
        lax.all_gather(value_weight, "ctx", axis=0, tiled=True),
        lax.all_gather(out_weight, "ctx", axis=0, tiled=True),
        lax.all_gather(in_weight, "ctx", axis=0, tiled=True),
        lax.all_gather(down_weight, "ctx", axis=0, tiled=True),
        lax.all_gather(query_bias, "ctx", axis=0, tiled=True),
        lax.all_gather(value_bias, "ctx", axis=0, tiled=True),
        lax.all_gather(out_bias, "ctx", axis=0, tiled=True),
        lax.all_gather(attn_norm_gain, "ctx", axis=0, tiled=True),
        lax.all_gather(attn_norm_bias, "ctx", axis=0, tiled=True),
        lax.all_gather(in_bias, "ctx", axis=0, tiled=True),
        lax.all_gather(down_bias, "ctx", axis=0, tiled=True),
        lax.all_gather(ffn_norm_gain, "ctx", axis=0, tiled=True),
        lax.all_gather(ffn_norm_bias, "ctx", axis=0, tiled=True),
    )
    full_mats = (
        lax.all_gather(row_parts[0], "fsdp", axis=1, tiled=True),
        lax.all_gather(row_parts[1], "fsdp", axis=1, tiled=True),
        lax.all_gather(row_parts[2], "fsdp", axis=1, tiled=True),
        lax.all_gather(row_parts[3], "fsdp", axis=1, tiled=True),
        lax.all_gather(row_parts[4], "fsdp", axis=1, tiled=True),
        lax.all_gather(row_parts[5], "fsdp", axis=1, tiled=True),
    )
    query_full, key_full, value_full, out_full, in_full, down_full = full_mats
    query_vec = row_parts[6].astype(jnp.float32)
    value_vec = row_parts[7].astype(jnp.float32)
    out_vec = row_parts[8].astype(jnp.float32)
    gain_one = row_parts[9].astype(jnp.float32)
    bias_one = row_parts[10].astype(jnp.float32)
    in_vec = row_parts[11].astype(jnp.float32)
    down_vec = row_parts[12].astype(jnp.float32)
    gain_two = row_parts[13].astype(jnp.float32)
    bias_two = row_parts[14].astype(jnp.float32)
    local_slots = ctx_index * slot_count + jnp.arange(slot_count)
    local_ok = local_slots[None, :] < lengths[:, None]
    valid_mask = local_ok.astype(jnp.float32)
    valid_col = valid_mask.reshape(row_count, 1)
    key_ok = jnp.arange(slot_count * ctx_size)[None, :] < lengths[:, None]
    token_rows = tokens.reshape(row_count, model_width)
    queries_b = (plain_product(token_rows, query_full) + query_vec).astype(jnp.bfloat16)
    keys_b = plain_product(token_rows, key_full).astype(jnp.bfloat16)
    values_b = (plain_product(token_rows, value_full) + value_vec).astype(jnp.bfloat16)
    pair_local = jnp.concatenate([keys_b, values_b], axis=1).reshape(
        seq_count, slot_count, 2 * model_width
    )
    pair_all = lax.all_gather(pair_local, "ctx", axis=1, tiled=True)
    query_seq = queries_b.reshape(seq_count, slot_count, model_width)
    mixed_out, log_totals = attend(query_seq, pair_all, key_ok)
    mixed_b = mixed_out.reshape(row_count, model_width).astype(jnp.bfloat16)
    attn_branch = plain_product(mixed_b, out_full) + out_vec
    stream = token_rows.astype(jnp.float32) + attn_branch
    norm_one, norm_one_back = jax.vjp(layer_norm, stream, gain_one, bias_one)
    norm_one_b = norm_one.astype(jnp.bfloat16)
    inner_pre = plain_product(norm_one_b, in_full) + in_vec
    act_out, gelu_back = jax.vjp(gelu_exact, inner_pre)
    act_b = act_out.astype(jnp.bfloat16)
    ffn_branch = plain_product(act_b, down_full) + down_vec
    stream_two = norm_one + ffn_branch
    final_out, norm_two_back = jax.vjp(layer_norm, stream_two, gain_two, bias_two)
    layer_out = (
        (valid_col * final_out).astype(jnp.bfloat16).reshape(seq_count, slot_count, model_width)
    )
    grad_final = valid_col * cotangent.reshape(row_count, model_width).astype(jnp.float32)
    grad_stream_two, grad_gain_two, grad_bias_two = norm_two_back(grad_final)
    grad_ffn_b = grad_stream_two.astype(jnp.bfloat16)
    grad_down_vec = column_sums(grad_ffn_b)
    grad_down_full = row_product(act_b, grad_ffn_b)
    grad_inner_b = gelu_back(column_product(grad_ffn_b, down_full))[0].astype(jnp.bfloat16)
    grad_in_vec = column_sums(grad_inner_b)
    grad_in_full = row_product(norm_one_b, grad_inner_b)
    grad_norm_one = grad_stream_two + column_product(grad_inner_b, in_full)
    grad_stream, grad_gain_one, grad_bias_one = norm_one_back(grad_norm_one)
    grad_attn_b = grad_stream.astype(jnp.bfloat16)
    grad_out_vec = column_sums(grad_attn_b)
    grad_out_full = row_product(mixed_b, grad_attn_b)
    grad_mixed = (
        column_product(grad_attn_b, out_full)
        .astype(jnp.bfloat16)
        .reshape(seq_count, slot_count, model_width)
    )
    grad_query_seq, grad_pair = attend_back(query_seq, pair_all, key_ok, log_totals, grad_mixed)
    grad_pair_local = lax.psum_scatter(
        grad_pair.astype(jnp.bfloat16), "ctx", scatter_dimension=1, tiled=True
    ).astype(jnp.float32)
    grad_keys_b = (
        grad_pair_local[:, :, :model_width].reshape(row_count, model_width).astype(jnp.bfloat16)
    )
    grad_values_b = (
        grad_pair_local[:, :, model_width:].reshape(row_count, model_width).astype(jnp.bfloat16)
    )
    grad_queries_b = grad_query_seq.reshape(row_count, model_width).astype(jnp.bfloat16)
    grad_query_full = row_product(token_rows, grad_queries_b)
    grad_query_vec = column_sums(grad_queries_b)
    grad_key_full = row_product(token_rows, grad_keys_b)
    grad_value_full = row_product(token_rows, grad_values_b)
    grad_value_vec = column_sums(grad_values_b)
    tokens_grad = (
        (
            grad_stream
            + column_product(grad_queries_b, query_full)
            + column_product(grad_keys_b, key_full)
            + column_product(grad_values_b, value_full)
        )
        .astype(jnp.bfloat16)
        .reshape(seq_count, slot_count, model_width)
    )
    narrow = (
        lax.psum_scatter(
            grad_query_full.astype(jnp.bfloat16), "fsdp", scatter_dimension=1, tiled=True
        ).astype(jnp.float32),
        lax.psum_scatter(
            grad_key_full.astype(jnp.bfloat16), "fsdp", scatter_dimension=1, tiled=True
        ).astype(jnp.float32),
        lax.psum_scatter(
            grad_value_full.astype(jnp.bfloat16), "fsdp", scatter_dimension=1, tiled=True
        ).astype(jnp.float32),
        lax.psum_scatter(
            grad_out_full.astype(jnp.bfloat16), "fsdp", scatter_dimension=1, tiled=True
        ).astype(jnp.float32),
        lax.psum_scatter(
            grad_in_full.astype(jnp.bfloat16), "fsdp", scatter_dimension=1, tiled=True
        ).astype(jnp.float32),
        lax.psum_scatter(
            grad_down_full.astype(jnp.bfloat16), "fsdp", scatter_dimension=1, tiled=True
        ).astype(jnp.float32),
    )
    owned_grads = (
        lax.psum_scatter(
            narrow[0].astype(jnp.bfloat16), "ctx", scatter_dimension=0, tiled=True
        ).astype(jnp.float32),
        lax.psum_scatter(
            narrow[1].astype(jnp.bfloat16), "ctx", scatter_dimension=0, tiled=True
        ).astype(jnp.float32),
        lax.psum_scatter(
            narrow[2].astype(jnp.bfloat16), "ctx", scatter_dimension=0, tiled=True
        ).astype(jnp.float32),
        lax.psum_scatter(
            narrow[3].astype(jnp.bfloat16), "ctx", scatter_dimension=0, tiled=True
        ).astype(jnp.float32),
        lax.psum_scatter(
            narrow[4].astype(jnp.bfloat16), "ctx", scatter_dimension=0, tiled=True
        ).astype(jnp.float32),
        lax.psum_scatter(
            narrow[5].astype(jnp.bfloat16), "ctx", scatter_dimension=0, tiled=True
        ).astype(jnp.float32),
    )
    moments = jnp.stack(
        [
            jnp.sum(valid_col * stream * stream),
            jnp.sum(valid_col * attn_branch * attn_branch),
            jnp.sum(valid_col * ffn_branch * ffn_branch),
            jnp.sum(valid_col),
        ]
    )
    summed = lax.psum(
        (
            moments,
            grad_query_vec,
            grad_value_vec,
            grad_out_vec,
            grad_gain_one,
            grad_bias_one,
            grad_in_vec,
            grad_down_vec,
            grad_gain_two,
            grad_bias_two,
        ),
        ("ctx", "fsdp"),
    )
    width_shard = query_bias.shape[0]
    hidden_shard = in_bias.shape[0]

    def own_piece(vector_full, shard_len):
        return lax.dynamic_slice_in_dim(vector_full, ctx_index * shard_len, shard_len, 0)

    rms_values = jnp.sqrt(summed[0][:3] / (summed[0][3] * model_width))
    return (
        layer_out,
        tokens_grad,
        owned_grads[0],
        owned_grads[1],
        owned_grads[2],
        owned_grads[3],
        owned_grads[4],
        owned_grads[5],
        own_piece(summed[1], width_shard),
        own_piece(summed[2], width_shard),
        own_piece(summed[3], width_shard),
        own_piece(summed[4], width_shard),
        own_piece(summed[5], width_shard),
        own_piece(summed[6], hidden_shard),
        own_piece(summed[7], width_shard),
        own_piece(summed[8], width_shard),
        own_piece(summed[9], width_shard),
        rms_values,
    )


HEADS_HERE = 3
HEAD_COLS = HEADS_HERE * HEAD_DIM
rows_first = (((0,), (0,)), ((), ()))
lanes_both = (((1,), (1,)), ((), ()))
plain_contract = (((1,), (0,)), ((), ()))


def effort(microseconds):
    return pl.CostEstimate(
        flops=int(microseconds * 1e8), transcendentals=0, bytes_accessed=int(microseconds * 1e5)
    )


kernel_params = pltpu.CompilerParams(vmem_limit_bytes=24 * 1024 * 1024)


def product32(left_side, right_side, contract):
    return lax.dot_general(left_side, right_side, contract, preferred_element_type=jnp.float32)


def ctx_move(value, mask):
    return lax.ppermute(value, "ctx", [(i, i ^ mask) for i in range(16)])


def core_swap(value):
    return ctx_move(value, 1)


def y_swap(value):
    return ctx_move(value, 2)


def x_swap(value):
    return lax.ppermute(value, "fsdp", [(0, 1), (1, 0)])


def add_b(left_side, right_side):
    return (left_side.astype(jnp.float32) + right_side.astype(jnp.float32)).astype(jnp.bfloat16)


def row_sums(matrix_b):
    return jnp.sum(matrix_b.astype(jnp.float32), axis=0, keepdims=True)


def hold(*values):
    return lax.optimization_barrier(values)


def when_flag(flag_ref, run, idle):
    if flag_ref is None:
        run()
    else:
        pl.when(flag_ref[0] > 0)(run)
        pl.when(flag_ref[0] <= 0)(idle)


def attend_kernel(count, first, last, flagged, *refs):
    flag_ref = refs[0] if flagged else None
    refs = refs[flagged:]
    query_ref, pairs = refs[0], refs[1 : 1 + count]
    refs = refs[1 + count :]
    if not first:
        peak_in, total_in, mixed_in = refs[:3]
        refs = refs[3:]

    def one_head(head, carry):
        key_rows = pl.ds(pl.multiple_of(head * HEAD_DIM, HEAD_DIM), HEAD_DIM)
        value_rows = pl.ds(pl.multiple_of(HEAD_COLS + head * HEAD_DIM, HEAD_DIM), HEAD_DIM)
        query = query_ref[key_rows, :]
        width = query.shape[1]
        if first:
            peak = jnp.full((1, width), -1e30, jnp.float32)
            total = jnp.zeros((1, width), jnp.float32)
            mixed = jnp.zeros((HEAD_DIM, width), jnp.float32)
        else:
            peak, total, mixed = peak_in[head][0:1], total_in[head][0:1], mixed_in[key_rows, :]
        for pair in pairs:
            scores = product32(pair[key_rows, :], query, rows_first)
            new_peak = jnp.maximum(peak, jnp.max(scores, axis=0, keepdims=True))
            expo = jnp.exp(scores - new_peak)
            shrink = jnp.exp(peak - new_peak)
            total = total * shrink + jnp.sum(expo, axis=0, keepdims=True)
            mixed = mixed * shrink + product32(
                pair[value_rows, :], expo.astype(jnp.bfloat16), plain_contract
            )
            peak = new_peak
        if last:
            mixed_out, log_out = refs
            mixed_out[key_rows, :] = (mixed / total).astype(jnp.bfloat16)
            log_out[head] = jnp.broadcast_to(peak + jnp.log(total), (8, width))
        else:
            peak_out, total_out, sum_out = refs
            peak_out[head] = jnp.broadcast_to(peak, (8, width))
            total_out[head] = jnp.broadcast_to(total, (8, width))
            sum_out[key_rows, :] = mixed
        return carry

    def run():
        lax.fori_loop(0, HEADS_HERE, one_head, 0)

    def idle():
        for ref in refs:
            ref[...] = jnp.zeros_like(ref)

    when_flag(flag_ref, run, idle)


def attend_call(query, pairs, state=None, last=False, flag=None):
    width = query.shape[1]
    stat = jax.ShapeDtypeStruct((HEADS_HERE, 8, width), jnp.float32)
    if last:
        outs = [jax.ShapeDtypeStruct((HEAD_COLS, width), jnp.bfloat16), stat]
    else:
        outs = [stat, stat, jax.ShapeDtypeStruct((HEAD_COLS, width), jnp.float32)]
    ins = [query, *pairs, *(() if state is None else state)]
    specs = [pl.BlockSpec(memory_space=pltpu.VMEM)] * len(ins)
    if flag is not None:
        ins, specs = [flag, *ins], [pl.BlockSpec(memory_space=pltpu.SMEM), *specs]
    return pl.pallas_call(
        functools.partial(attend_kernel, len(pairs), state is None, last, int(flag is not None)),
        out_shape=outs,
        in_specs=specs,
        compiler_params=kernel_params,
        cost_estimate=effort(3.5),
    )(*ins)


def attend_back_kernel(count, first, flagged, *refs):
    flag_ref = refs[0] if flagged else None
    refs = refs[flagged:]
    query_ref, grad_ref, log_ref, mixed_ref = refs[:4]
    pairs = refs[4 : 4 + count]
    refs = refs[4 + count :]
    if not first:
        grad_query_in, refs = refs[0], refs[1:]
    grad_query_out, grad_pairs = refs[0], refs[1 : 1 + count]
    held, sems = refs[1 + count :]
    hbm_pairs, pairs = pairs, [held.at[i] for i in range(count)]

    def one_head(head, carry):
        key_rows = pl.ds(pl.multiple_of(head * HEAD_DIM, HEAD_DIM), HEAD_DIM)
        value_rows = pl.ds(pl.multiple_of(HEAD_COLS + head * HEAD_DIM, HEAD_DIM), HEAD_DIM)
        query, grad = query_ref[key_rows, :], grad_ref[key_rows, :]
        log_row = log_ref[head][0:1]
        inner = jnp.sum(
            mixed_ref[key_rows, :].astype(jnp.float32) * grad.astype(jnp.float32),
            axis=0,
            keepdims=True,
        )
        if first:
            grad_query = jnp.zeros((HEAD_DIM, query.shape[1]), jnp.float32)
        else:
            grad_query = grad_query_in[key_rows, :]
        for pair, grad_pair in zip(pairs, grad_pairs):
            keys = pair[key_rows, :]
            probs = jnp.exp(product32(keys, query, rows_first) - log_row)
            grad_probs = product32(pair[value_rows, :], grad, rows_first)
            grad_scores = (probs * (grad_probs - inner)).astype(jnp.bfloat16)
            grad_query = grad_query + product32(keys, grad_scores, plain_contract)
            grad_pair[key_rows, :] = product32(query, grad_scores, lanes_both).astype(jnp.bfloat16)
            grad_pair[value_rows, :] = product32(
                grad, probs.astype(jnp.bfloat16), lanes_both
            ).astype(jnp.bfloat16)
        grad_query_out[key_rows, :] = grad_query
        return carry

    def run():
        copies = [
            pltpu.make_async_copy(hbm, held.at[i], sems.at[i]) for i, hbm in enumerate(hbm_pairs)
        ]
        for copy in copies:
            copy.start()
        for copy in copies:
            copy.wait()
        lax.fori_loop(0, HEADS_HERE, one_head, 0)

    def idle():
        for ref in (grad_query_out, *grad_pairs):
            ref[...] = jnp.zeros_like(ref)

    when_flag(flag_ref, run, idle)


def attend_back_call(query, grad, log_rows, mixed, pairs, grad_query=None, flag=None):
    outs = [jax.ShapeDtypeStruct(query.shape, jnp.float32)]
    outs += [jax.ShapeDtypeStruct(pair.shape, jnp.bfloat16) for pair in pairs]
    ins = [query, grad, log_rows, mixed, *pairs, *(() if grad_query is None else (grad_query,))]
    specs = [pl.BlockSpec(memory_space=pltpu.VMEM)] * len(ins)
    specs[4 : 4 + len(pairs)] = [pl.BlockSpec(memory_space=pl.ANY)] * len(pairs)
    if flag is not None:
        ins, specs = [flag, *ins], [pl.BlockSpec(memory_space=pltpu.SMEM), *specs]
    return pl.pallas_call(
        functools.partial(
            attend_back_kernel, len(pairs), grad_query is None, int(flag is not None)
        ),
        out_shape=outs,
        in_specs=specs,
        scratch_shapes=[
            pltpu.VMEM((len(pairs), *pairs[0].shape), jnp.bfloat16),
            pltpu.SemaphoreType.DMA((len(pairs),)),
        ],
        compiler_params=kernel_params,
        cost_estimate=effort(10.0),
    )(*ins)


def pack_kernel(me_ref, *refs):
    given, (rows_ref, keep_ref, send_ref, in_keep, in_send) = refs[:4], refs[4:9]
    held, sems = refs[9:13], refs[13]
    copies = [
        pltpu.make_async_copy(source, target, sems.at[i])
        for i, (source, target) in enumerate(zip(given, held))
    ]
    for copy in copies:
        copy.start()
    for copy in copies:
        copy.wait()
    y_low, core_low = (me_ref[0] & 2) == 0, (me_ref[0] & 1) == 0
    for i, ref in enumerate(held[:3]):
        low, high = ref[:, :192], ref[:, 192:]
        keep_ref[0:48, 192 * i : 192 * (i + 1)] = jnp.where(y_low, low, high)
        send_ref[0:48, 192 * i : 192 * (i + 1)] = jnp.where(y_low, high, low)
    keep_ref[48:56, :] = rows_ref[...]
    send_ref[48:56, :] = rows_ref[...]
    for k in range(4):
        even = held[3][:, 384 * k : 384 * k + 192]
        odd = held[3][:, 384 * k + 192 : 384 * (k + 1)]
        in_keep[:, 192 * k : 192 * (k + 1)] = jnp.where(core_low, even, odd)
        in_send[:, 192 * k : 192 * (k + 1)] = jnp.where(core_low, odd, even)


def pack_call(me, weights, rows):
    return pl.pallas_call(
        pack_kernel,
        out_shape=[
            jax.ShapeDtypeStruct(shape, jnp.bfloat16)
            for shape in ((56, 576), (56, 576), (48, 768), (48, 768))
        ],
        in_specs=[
            pl.BlockSpec(memory_space=pltpu.SMEM),
            *[pl.BlockSpec(memory_space=pl.ANY)] * 4,
            pl.BlockSpec(memory_space=pltpu.VMEM),
        ],
        scratch_shapes=[
            *(pltpu.VMEM(weight.shape, jnp.bfloat16) for weight in weights),
            pltpu.SemaphoreType.DMA((4,)),
        ],
        compiler_params=kernel_params,
        cost_estimate=effort(400.0),
    )(me, *weights, rows)


def place_qkv_kernel(me_ref, own_ref, far_ref, mats_ref, wide_ref, heads_ref, hidden_ref, vecs_ref):
    for core, stack in enumerate((own_ref, far_ref)):
        for z in range(4):
            for y in range(2):
                owner = jnp.bitwise_xor(me_ref[0], z * 4 + y * 2 + core)
                mats_ref[owner] = stack[z, y, 0:48]
                vecs_ref[owner] = stack[z, y, 48:56].astype(jnp.float32)
    core_low = (me_ref[0] & 1) == 0
    for i in range(16):
        wide_ref[:, 48 * i : 48 * (i + 1)] = vecs_ref[i, :, 0:48]
    for i in range(8):
        hidden_ref[:, 192 * i : 192 * (i + 1)] = jnp.where(
            core_low, vecs_ref[2 * i, :, 128:320], vecs_ref[2 * i + 1, :, 128:320]
        )
    column = 2 * me_ref[1] + ((me_ref[0] >> 1) & 1)
    for i in range(4):

        @pl.when(column == i)
        def _():
            heads_ref[...] = wide_ref[:, 192 * i : 192 * (i + 1)]


def place_in_kernel(me_ref, one_own, one_far, two_own, two_far, in_ref, out_ref):
    zy_at, x_low = me_ref[0] >> 1, me_ref[1] == 0
    for y, stack in enumerate((two_own, two_far)):
        for z in range(4):
            owner = jnp.bitwise_xor(zy_at, z * 2 + y)
            own, far = one_own[4 * y + z], one_far[4 * y + z]
            low, high = jnp.where(x_low, own, far), jnp.where(x_low, far, own)
            in_ref[owner, :, 0:384], in_ref[owner, :, 768:1152] = low[0:96], high[0:96]
            out_ref[owner, :, 0:384], out_ref[owner, :, 384:768] = low[96:144], high[96:144]
            own, far = stack[0, z], stack[1, z]
            in_ref[owner, :, 384:768] = jnp.where(x_low, own, far)
            in_ref[owner, :, 1152:1536] = jnp.where(x_low, far, own)


def place_down_kernel(me_ref, one_own, one_far, two_own, two_far, down_ref):
    zy_at, x_low = me_ref[0] >> 1, me_ref[1] == 0
    for y, stack in enumerate((two_own, two_far)):
        for z in range(4):
            owner = jnp.bitwise_xor(zy_at, z * 2 + y)
            own, far = one_own[4 * y + z], one_far[4 * y + z]
            down_ref[owner, 0:96, 0:384] = jnp.where(x_low, own, far)
            down_ref[owner, 0:96, 384:768] = jnp.where(x_low, far, own)
            own, far = stack[0, z], stack[1, z]
            down_ref[owner, 96:192, 0:384] = jnp.where(x_low, own, far)
            down_ref[owner, 96:192, 384:768] = jnp.where(x_low, far, own)


def vectors_kernel(me_ref, *refs):
    rows, (query_ref, hidden_ref), moments, out_ref = refs[:7], refs[7:9], refs[9:13], refs[13]
    out_ref[...] = jnp.zeros_like(out_ref)
    core = me_ref[0] & 1
    column = 2 * me_ref[1] + ((me_ref[0] >> 1) & 1)
    totals = [jnp.sum(ref[...], axis=1, keepdims=True) for ref in moments]
    for i in range(16):
        for row, ref in enumerate(rows):
            out_ref[i, row : row + 1, 0:48] = ref[0:1, 48 * i : 48 * (i + 1)]
        part = query_ref[0:1, 48 * (i % 4) : 48 * (i % 4 + 1)]
        out_ref[i, 7:8, 0:48] = jnp.where(column == i // 4, part, 0.0)
        part = hidden_ref[0:1, 192 * (i // 2) : 192 * (i // 2 + 1)]
        out_ref[i, 0:1, 128:320] = jnp.where(core == i % 2, part, 0.0)
        for row, total in enumerate(totals):
            out_ref[i, row + 1 : row + 2, 128:256] = jnp.broadcast_to(total, (1, 128))


def place_call(kernel, me, stacks, shapes, more=(), scratch=(), cost=2.0):
    return pl.pallas_call(
        kernel,
        out_shape=[jax.ShapeDtypeStruct(shape, jnp.bfloat16) for shape in shapes]
        + [jax.ShapeDtypeStruct(shape, jnp.float32) for shape in more],
        scratch_shapes=[pltpu.VMEM(shape, jnp.float32) for shape in scratch],
        in_specs=[pl.BlockSpec(memory_space=pltpu.SMEM)]
        + [pl.BlockSpec(memory_space=pltpu.VMEM)] * len(stacks),
        compiler_params=kernel_params,
        cost_estimate=effort(cost),
    )(me, *stacks)


def fast_body(
    tokens,
    lengths,
    cotangent,
    query_weight,
    key_weight,
    value_weight,
    out_weight,
    in_weight,
    down_weight,
    query_bias,
    value_bias,
    out_bias,
    attn_norm_gain,
    attn_norm_bias,
    in_bias,
    down_bias,
    ffn_norm_gain,
    ffn_norm_bias,
):
    slot_count, width = tokens.shape[1:]
    me = lax.axis_index("ctx")
    x_at = lax.axis_index("fsdp")
    z_at, y_at, core_at = me >> 2, (me >> 1) & 1, me & 1
    y_low, x_low, core_low = y_at == 0, x_at == 0, core_at == 0
    own_long = lengths[0] == slot_count * lax.axis_size("ctx")
    short_flag = (z_at == 0).astype(jnp.int32).reshape(1)

    half = HEAD_COLS
    vector_rows = sum(
        lax.pad(piece[None, :], jnp.asarray(0, jnp.bfloat16), ((row, 7 - row, 0), (at, 576 - at - piece.shape[0], 0)))
        for row, at, piece in (
            (0, 0, query_bias),
            (1, 0, value_bias),
            (2, 0, out_bias),
            (3, 0, attn_norm_gain),
            (4, 0, attn_norm_bias),
            (5, 0, down_bias),
            (6, 0, ffn_norm_gain),
            (7, 0, ffn_norm_bias),
            (0, 128, in_bias),
        )
    )
    where_me = jnp.stack([me, x_at]).astype(jnp.int32)
    keep_cols, send_cols, in_keep, in_send = pack_call(
        where_me, (query_weight, key_weight, value_weight, in_weight), vector_rows
    )
    token_rows = tokens[0]
    in_got = core_swap(in_send)
    in_block = jnp.concatenate(
        [jnp.where(core_low, in_keep, in_got), jnp.where(core_low, in_got, in_keep)], axis=0
    )
    ffn_block = jnp.concatenate([in_block[:, :384], out_weight, in_block[:, 384:], down_weight])
    other_rows = x_swap(token_rows)
    long_own = jnp.where(own_long, token_rows, other_rows)
    short_own = jnp.where(own_long, other_rows, token_rows)
    got_cols, ffn_one, long_own, short_own = hold(
        y_swap(send_cols), ctx_move(ffn_block, 4), long_own, short_own
    )
    own_block = jnp.stack([keep_cols, got_cols])
    ffn_two = ctx_move(ffn_block, 8)
    z_one, z_two, long_far, short_own = hold(
        ctx_move(own_block, 4), ctx_move(own_block, 8), y_swap(long_own), short_own
    )
    z_three, ffn_two = hold(ctx_move(z_two, 4), ffn_two)
    ffn_three = ctx_move(ffn_two, 4)
    z_stack = jnp.stack([own_block, z_one, z_two, z_three])
    qkv_weight, wide, heads, hidden = place_call(
        place_qkv_kernel,
        where_me,
        (z_stack, core_swap(z_stack)),
        ((16, 48, 576),),
        ((8, 768), (8, half), (8, 1536)),
        ((16, 8, 576),),
    )
    qkv_weight = qkv_weight.reshape(768, 576)
    out_vec, gain_one, bias_one, down_vec, gain_two, bias_two = (
        wide[row : row + 1] for row in range(2, 8)
    )
    in_vec = hidden[:1]
    columns = heads.T
    query_add, value_add = columns[:, 0:1], columns[:, 1:2]
    pair_add = jnp.concatenate([jnp.zeros_like(value_add), value_add], axis=0)

    long_rows = jnp.concatenate([long_own, long_far], axis=0)
    def project(rows):
        query = product32(qkv_weight[:, :half], rows, (((0,), (1,)), ((), ()))) + query_add
        pair = product32(qkv_weight[:, half:], rows, (((0,), (1,)), ((), ()))) + pair_add
        scale = jnp.asarray(score_scale, jnp.bfloat16)
        return query.astype(jnp.bfloat16) * scale, pair.astype(jnp.bfloat16)

    long_query, long_pair = project(long_rows)
    kv_two, kv_one = ctx_move(long_pair, 8), ctx_move(long_pair, 4)
    long_pair_far = core_swap(long_pair)
    short_own, long_pair_far = hold(short_own, long_pair_far)
    short_far = y_swap(short_own)
    state = attend_call(long_query, (long_pair, long_pair_far))
    short_rows = jnp.concatenate([short_own, short_far], axis=0)
    short_query, short_pair = project(short_rows)
    short_pairs = (short_pair, core_swap(short_pair))
    short_mixed, short_log = attend_call(short_query, short_pairs, last=True, flag=short_flag)
    ffn_stack = jnp.stack([ffn_block, ffn_one, ffn_two, ffn_three])
    in_one, in_two = ffn_stack[:, :144], ffn_stack[:, 144:240]
    in_one_y, in_two_x = y_swap(in_one), x_swap(in_two)
    kv_one, kv_two, in_one_y, in_two_x, short_mixed, *state = hold(
        kv_one, kv_two, in_one_y, in_two_x, short_mixed, *state
    )
    kv_three = ctx_move(kv_two, 4)
    in_one, in_two = jnp.concatenate([in_one, in_one_y], axis=0), jnp.stack([in_two, in_two_x])
    in_one_far, in_two_far = x_swap(in_one), y_swap(in_two)
    kv_one_far, kv_two_far = core_swap(kv_one), core_swap(kv_two)
    state = attend_call(long_query, (kv_one, kv_one_far), state)
    state = attend_call(long_query, (kv_two, kv_two_far), state)
    kv_three, *state = hold(kv_three, *state)
    kv_three_far = core_swap(kv_three)
    long_mixed, long_log = attend_call(long_query, (kv_three, kv_three_far), state, last=True)
    pairs = (
        (long_pair, long_pair_far),
        (kv_one, kv_one_far),
        (kv_two, kv_two_far),
        (kv_three, kv_three_far),
    )

    rows_here = slot_count
    sent = jnp.concatenate([long_mixed[:, rows_here:], short_mixed[:, rows_here:]], axis=0)
    sent, in_one_far, in_two_far = hold(sent, in_one_far, in_two_far)
    got = y_swap(sent)
    def by_y(mine, theirs):
        return jnp.concatenate(
            [jnp.where(y_low, mine, theirs), jnp.where(y_low, theirs, mine)], axis=0
        )

    long_heads = by_y(long_mixed[:, :rows_here], got[:half])
    short_heads = by_y(short_mixed[:, :rows_here], got[half:])
    own_heads = jnp.where(own_long, long_heads, short_heads)
    sent = jnp.where(own_long, short_heads, long_heads)
    far_heads = x_swap(sent)
    in_all, out_core = place_call(
        place_in_kernel,
        where_me,
        (in_one, in_one_far, in_two, in_two_far),
        ((8, 96, 1536), (8, 48, 768)),
    )
    down_one, down_two = ffn_stack[:, 240:336], ffn_stack[:, 336:]
    down_one, down_two, _ = hold(down_one, down_two, sent)
    down_one_y, down_two_x = hold(y_swap(down_one), x_swap(down_two))
    down_one = jnp.concatenate([down_one, down_one_y], axis=0)
    down_two = jnp.stack([down_two, down_two_x])
    (down_all,) = place_call(
        place_down_kernel,
        where_me,
        (down_one, x_swap(down_one), down_two, y_swap(down_two)),
        ((8, 192, 768),),
    )
    in_all, down_all = in_all.reshape(768, 1536), down_all.reshape(1536, 768)
    out_far = core_swap(out_core)
    out_all = jnp.stack(
        [jnp.where(core_low, out_core, out_far), jnp.where(core_low, out_far, out_core)], axis=1
    ).reshape(768, 768)

    mixed_t = jnp.concatenate(
        [jnp.where(x_low, own_heads, far_heads), jnp.where(x_low, far_heads, own_heads)], axis=0
    )

    local_slots = me * slot_count + jnp.arange(slot_count)
    valid_col = (local_slots < lengths[0]).astype(jnp.float32)[:, None]
    attn_branch = product32(mixed_t, out_all, rows_first) + out_vec
    stream = token_rows.astype(jnp.float32) + attn_branch
    norm_one, norm_one_back = jax.vjp(layer_norm, stream, gain_one, bias_one)
    norm_one_b = norm_one.astype(jnp.bfloat16)
    chip_norm = jnp.concatenate([norm_one_b, core_swap(norm_one_b)], axis=0)
    act_out, gelu_back = jax.vjp(gelu_exact, plain_product(chip_norm, in_all) + in_vec)
    act_b = act_out.astype(jnp.bfloat16)
    ffn_got = core_swap(plain_product(act_b[rows_here:], down_all).astype(jnp.bfloat16))
    ffn_part = plain_product(act_b[:rows_here], down_all)
    ffn_branch = ffn_part + ffn_got.astype(jnp.float32) + down_vec
    stream_two = norm_one + ffn_branch
    final_out, norm_two_back = jax.vjp(layer_norm, stream_two, gain_two, bias_two)
    layer_out = (valid_col * final_out).astype(jnp.bfloat16)[None]
    grad_final = valid_col * cotangent[0].astype(jnp.float32)
    grad_stream_two, grad_gain_two, grad_bias_two = norm_two_back(grad_final)
    grad_ffn_b = grad_stream_two.astype(jnp.bfloat16)
    grad_down_vec = row_sums(grad_ffn_b)
    chip_grad = jnp.concatenate([grad_ffn_b, core_swap(grad_ffn_b)], axis=0)
    grad_inner_b = gelu_back(column_product(chip_grad, down_all))[0].astype(jnp.bfloat16)
    grad_in_vec = row_sums(grad_inner_b)
    norm_got = core_swap(column_product(grad_inner_b[rows_here:], in_all).astype(jnp.bfloat16))
    norm_part = column_product(grad_inner_b[:rows_here], in_all)
    grad_norm_one = grad_stream_two + norm_part + norm_got.astype(jnp.float32)
    grad_stream, grad_gain_one, grad_bias_one = norm_one_back(grad_norm_one)
    grad_attn_b = grad_stream.astype(jnp.bfloat16)
    grad_out_vec = row_sums(grad_attn_b)
    grad_mixed_t = product32(out_all, grad_attn_b, lanes_both).astype(jnp.bfloat16)
    ones = jnp.ones((8, slot_count), jnp.bfloat16)
    grad_value_vec = product32(ones, grad_mixed_t, lanes_both)[:1]

    chip_norm, act_b, grad_inner_b, mixed_w, _ = lax.optimization_barrier(
        (chip_norm, act_b, grad_inner_b, mixed_t, grad_mixed_t)
    )
    inner_send = jnp.where(x_low, grad_inner_b[:, 768:], grad_inner_b[:, :768])
    inner_keep = jnp.where(x_low, grad_inner_b[:, :768], grad_inner_b[:, 768:])
    def with_out(in_part, out_part):
        in_part = in_part.astype(jnp.bfloat16).reshape(4, 2, 96, 768)
        return jnp.concatenate([in_part[..., :384], in_part[..., 384:], out_part], axis=2)

    grad_out = plain_product(mixed_w, grad_attn_b).astype(jnp.bfloat16).reshape(4, 2, 2, 48, 768)
    out_sum = add_b(
        jnp.where(core_low, grad_out[:, :, 0], grad_out[:, :, 1]),
        core_swap(jnp.where(core_low, grad_out[:, :, 1], grad_out[:, :, 0])),
    )
    in_send = with_out(
        row_product(chip_norm, inner_send),
        jnp.where(x_low, out_sum[..., 384:], out_sum[..., :384]),
    )
    in_keep_grad = with_out(
        row_product(chip_norm, inner_keep),
        jnp.where(x_low, out_sum[..., :384], out_sum[..., 384:]),
    )
    grad_down = row_product(act_b, chip_grad).astype(jnp.bfloat16).reshape(4, 2, 192, 768)
    down_send = jnp.where(y_low, grad_down[:, 1], grad_down[:, 0])
    down_keep = jnp.where(y_low, grad_down[:, 0], grad_down[:, 1])
    keep_x = jnp.where(x_low, grad_mixed_t[:384], grad_mixed_t[384:])
    got_x = x_swap(jnp.where(x_low, grad_mixed_t[384:], grad_mixed_t[:384]))
    long_x = jnp.where(own_long, keep_x, got_x)
    short_x = jnp.where(own_long, got_x, keep_x)
    both_keep = jnp.where(y_low, long_x[:half], long_x[half:])
    short_keep = jnp.where(y_low, short_x[:half], short_x[half:])
    sent = jnp.concatenate(
        [
            jnp.where(y_low, long_x[half:], long_x[:half]),
            jnp.where(y_low, short_x[half:], short_x[:half]),
        ],
        axis=0,
    )
    got = y_swap(sent)
    long_grad = jnp.concatenate([both_keep, got[:half]], axis=1)
    short_grad = jnp.concatenate([short_keep, got[half:]], axis=1)
    in_send, down_send, long_grad, _ = hold(in_send, down_send, long_grad, got)
    in_x, down_y = x_swap(in_send), y_swap(down_send)


    grad_query, *grads = attend_back_call(
        long_query, long_grad, long_log, long_mixed, sum(pairs[::-1], ())
    )
    near, far = grads[::2], grads[1::2]
    short_query_b, grad_query = hold(short_query, grad_query)
    short_back = attend_back_call(
        short_query_b,
        short_grad,
        short_log,
        short_mixed,
        short_pairs,
        flag=short_flag,
    )
    *far, grad_query, in_x, down_y, short_query_g, short_near, short_far = hold(
        *(core_swap(part) for part in far), grad_query, in_x, down_y, *short_back
    )
    three, two, one = (add_b(near[i], far[i]) for i in range(3))
    near_own, far_own = near[3], far[3]
    in_sum = add_b(in_keep_grad, in_x)
    down_sum = add_b(down_keep, down_y)
    three_hop, one_got = ctx_move(three, 4), ctx_move(one, 4)
    two_got = ctx_move(add_b(two, three_hop), 8)
    in_send = jnp.where(y_low, in_sum[:, 1], in_sum[:, 0])
    down_send = jnp.where(x_low, down_sum[..., 384:], down_sum[..., :384])
    in_send, down_send, short_far = hold(in_send, down_send, short_far)
    in_y, down_x = y_swap(in_send), x_swap(down_send)
    short_pair_grad = add_b(short_near, core_swap(short_far))
    stream, attn_branch, ffn_branch, in_y = hold(stream, attn_branch, ffn_branch, in_y)
    (
        grad_value_vec,
        grad_out_vec,
        grad_gain_one,
        grad_bias_one,
        grad_down_vec,
        grad_gain_two,
        grad_bias_two,
        grad_in_vec,
        in_y,
    ) = hold(
        grad_value_vec,
        grad_out_vec,
        grad_gain_one,
        grad_bias_one,
        grad_down_vec,
        grad_gain_two,
        grad_bias_two,
        grad_in_vec,
        in_y,
    )
    long_query_grad = (grad_query * score_scale).astype(jnp.bfloat16)
    short_query_grad = (short_query_g * score_scale).astype(jnp.bfloat16)
    ones_wide = jnp.ones((8, 2 * slot_count), jnp.bfloat16)
    query_sums = product32(ones_wide, long_query_grad, lanes_both) + product32(
        ones_wide, short_query_grad, lanes_both
    )
    (owner_sums,) = place_call(
        vectors_kernel,
        where_me,
        (
            grad_value_vec,
            grad_out_vec,
            grad_gain_one,
            grad_bias_one,
            grad_down_vec,
            grad_gain_two,
            grad_bias_two,
            query_sums,
            grad_in_vec,
            jnp.sum(valid_col * stream * stream, axis=0, keepdims=True),
            jnp.sum(valid_col * attn_branch * attn_branch, axis=0, keepdims=True),
            jnp.sum(valid_col * ffn_branch * ffn_branch, axis=0, keepdims=True),
            jnp.broadcast_to(jnp.sum(valid_col, axis=0, keepdims=True) / 128, (1, 128)),
        ),
        (),
        ((16, 8, 384),),
    )
    owner_sums = owner_sums.astype(jnp.bfloat16)
    owner_sums = add_b(owner_sums, x_swap(owner_sums)).reshape(4, 2, 2, 8, 384)
    owner_sums = jnp.pad(owner_sums, ((0, 0), (0, 0), (0, 0), (0, 0), (0, 192)))

    def back_rows(grads):
        return product32(grads, qkv_weight, (((0,), (1,)), ((), ())))

    short_all = jnp.concatenate([short_query_grad, short_pair_grad], axis=0)
    short_rows_back = back_rows(short_all)
    short_got = y_swap(short_rows_back[rows_here:].astype(jnp.bfloat16))
    in_sum = add_b(jnp.where(y_low, in_sum[:, 0], in_sum[:, 1]), in_y)
    down_sum = add_b(jnp.where(x_low, down_sum[..., :384], down_sum[..., 384:]), down_x)
    ffn_sum = jnp.concatenate([in_sum, down_sum], axis=1)
    two_got, one_got, ffn_sum, owner_sums, short_got, short_rows_back = hold(
        two_got, one_got, ffn_sum, owner_sums, short_got, short_rows_back
    )
    long_pair_grad = near_own.astype(jnp.float32)
    for got_part in (far_own, one_got, two_got):
        long_pair_grad = long_pair_grad + got_part.astype(jnp.float32)
    long_pair_grad = long_pair_grad.astype(jnp.bfloat16)
    long_all = jnp.concatenate([long_query_grad, long_pair_grad], axis=0)
    long_back = back_rows(long_all)
    long_back, long_all = hold(long_back, long_all)
    long_got = y_swap(long_back[rows_here:].astype(jnp.bfloat16)).astype(jnp.float32)

    grad_qkv = product32(long_rows, long_all, (((0,), (1,)), ((), ()))) + product32(
        short_rows, short_all, (((0,), (1,)), ((), ()))
    )
    grad_qkv = grad_qkv.astype(jnp.bfloat16).reshape(4, 2, 2, 48, 576)
    grad_qkv = jnp.concatenate([grad_qkv, owner_sums], axis=3)
    core_keep = jnp.where(core_low, grad_qkv[:, :, 0], grad_qkv[:, :, 1])
    core_send = jnp.where(core_low, grad_qkv[:, :, 1], grad_qkv[:, :, 0])
    core_sum = add_b(core_keep, core_swap(core_send))

    def by_z(stack):
        return [
            lax.dynamic_index_in_dim(stack, z_at ^ mask, 0, keepdims=False) for mask in range(4)
        ]

    own_sum, one_part, two_part, three_part = by_z(core_sum)
    one_part, three_part = ctx_move(one_part, 4), ctx_move(three_part, 4)
    two_part, qkv_hop = hold(add_b(two_part, three_part), three_part)
    two_part = ctx_move(two_part, 8)
    own_sum = sum(part.astype(jnp.float32) for part in (own_sum, one_part, two_part))
    y_keep = jnp.where(y_low, own_sum[0], own_sum[1])
    y_got = y_swap(jnp.where(y_low, own_sum[1], own_sum[0]).astype(jnp.bfloat16))
    own_part, one_part, two_part, three_part = by_z(ffn_sum)
    one_part, _ = hold(one_part, qkv_hop)
    one_part = ctx_move(one_part, 4)
    two_part = ctx_move(add_b(two_part, ctx_move(three_part, 4)), 8)
    one_part, two_part, y_got = hold(one_part, two_part, y_got)
    ffn_owned = sum(part.astype(jnp.float32) for part in (own_part, one_part, two_part))
    y_got = y_got.astype(jnp.float32)
    vector_sums = y_keep[48:] + y_got[48:]
    y_keep, y_got = y_keep[:48], y_got[:48]
    low_part, high_part = jnp.where(y_low, y_keep, y_got), jnp.where(y_low, y_got, y_keep)
    owned_qkv = [
        jnp.concatenate(
            [low_part[:, half * i : half * (i + 1)], high_part[:, half * i : half * (i + 1)]],
            axis=1,
        )
        for i in range(3)
    ]

    in_owned = jnp.concatenate([ffn_owned[:96], ffn_owned[96:192]], axis=1)
    in_owned = in_owned.astype(jnp.bfloat16).reshape(2, 48, 768)
    in_mine = jnp.where(core_low, in_owned[0], in_owned[1])
    in_other = core_swap(jnp.where(core_low, in_owned[1], in_owned[0]))
    in_even = jnp.where(core_low, in_mine, in_other).astype(jnp.float32)
    in_odd = jnp.where(core_low, in_other, in_mine).astype(jnp.float32)
    owned_in = jnp.concatenate(
        [
            part[:, 192 * k : 192 * (k + 1)]
            for k in range(4)
            for part in (in_even, in_odd)
        ],
        axis=1,
    )
    owned_out, owned_down = ffn_owned[192:240], ffn_owned[240:]

    short_part = short_rows_back[:rows_here] + short_got.astype(jnp.float32)
    long_part = long_back[:rows_here] + long_got
    own_part = jnp.where(own_long, long_part, short_part)
    far_part = x_swap(jnp.where(own_long, short_part, long_part).astype(jnp.bfloat16))
    tokens_grad = (grad_stream + own_part + far_part.astype(jnp.float32)).astype(jnp.bfloat16)

    def own_piece(row):
        return vector_sums[row, :48]

    rms_values = jnp.sqrt(vector_sums[1:4, 128] / (vector_sums[4, 128] * width))
    return (
        layer_out,
        tokens_grad[None],
        owned_qkv[0],
        owned_qkv[1],
        owned_qkv[2],
        owned_out,
        owned_in,
        owned_down,
        vector_sums[7, :48],
        own_piece(0),
        own_piece(1),
        own_piece(2),
        own_piece(3),
        vector_sums[0, 128:320],
        own_piece(4),
        own_piece(5),
        own_piece(6),
        rms_values,
    )


def layer_body(tokens, *others):
    fits = lax.axis_size("ctx") == 16 and lax.axis_size("fsdp") == 2
    if fits and tokens.shape == (1, 256, 768):
        return fast_body(tokens, *others)
    return body(tokens, *others)


def solution(mesh):
    in_specs = (
        P("fsdp", "ctx", None),
        P("fsdp"),
        P("fsdp", "ctx", None),
        P("ctx", "fsdp"),
        P("ctx", "fsdp"),
        P("ctx", "fsdp"),
        P("ctx", "fsdp"),
        P("ctx", "fsdp"),
        P("ctx", "fsdp"),
        P("ctx"),
        P("ctx"),
        P("ctx"),
        P("ctx"),
        P("ctx"),
        P("ctx"),
        P("ctx"),
        P("ctx"),
        P("ctx"),
    )
    out_specs = (
        P("fsdp", "ctx", None),
        P("fsdp", "ctx", None),
        P("ctx", "fsdp"),
        P("ctx", "fsdp"),
        P("ctx", "fsdp"),
        P("ctx", "fsdp"),
        P("ctx", "fsdp"),
        P("ctx", "fsdp"),
        P("ctx"),
        P("ctx"),
        P("ctx"),
        P("ctx"),
        P("ctx"),
        P("ctx"),
        P("ctx"),
        P("ctx"),
        P("ctx"),
        P(),
    )
    return jax.shard_map(layer_body, mesh=mesh, in_specs=in_specs, out_specs=out_specs, check_vma=False)
```

profile of v0, /device:TPU:0, one launch (start us, length us, event | category | flops | bytes accessed | tf_op | source)
XLA Modules:
  0.0 326.0 jit_solution(5952822407867410124)
XLA Ops:
  7.1 2.6 collective-permute-start.3
  13.6 5.8 %collective-permute-done.3 = bf16[256,768]{1,0:T(8,128)(2,1)S(1)} collective-permute-done((bf16[256,768]{1,0:T(8,128)(2,1)S(1)}, bf16[256,768]{1,0:T(8,128)(2,1)S(1)}, u32[]{:S(2)}, u32[]{:S(2)}) %collective-permute-start.3) | collective-permute-done | bytes 393248 | tf_op jit(solution)/shard_map/ppermute | solution.py:386
  21.3 2.6 collective-permute-start.8
  25.9 9.2 %collective-permute-done.4 = bf16[2,56,576]{2,1,0:T(8,128)(2,1)S(1)} collective-permute-done((bf16[2,56,576]{2,1,0:T(8,128)(2,1)S(1)}, bf16[2,56,576]{2,1,0:T(8,128)(2,1)S(1)}, u32[]{:S(2)}, u32[]{:S(2)}) %collective-permute-start.4) | collective-permute-done | bytes 129056 | tf_op jit(solution)/shard_map/ppermute | solution.py:374
  35.2 9.4 %collective-permute-done.5 = bf16[2,56,576]{2,1,0:T(8,128)(2,1)S(1)} collective-permute-done((bf16[2,56,576]{2,1,0:T(8,128)(2,1)S(1)}, bf16[2,56,576]{2,1,0:T(8,128)(2,1)S(1)}, u32[]{:S(2)}, u32[]{:S(2)}) %collective-permute-start.5) | collective-permute-done | bytes 129056 | tf_op jit(solution)/shard_map/ppermute | solution.py:374
  45.2 4.4 %collective-permute-done.7 = bf16[2,56,576]{2,1,0:T(8,128)(2,1)S(1)} collective-permute-done((bf16[2,56,576]{2,1,0:T(8,128)(2,1)S(1)}, bf16[2,56,576]{2,1,0:T(8,128)(2,1)S(1)}, u32[]{:S(2)}, u32[]{:S(2)}) %collective-permute-start.7) | collective-permute-done | bytes 129056 | tf_op jit(solution)/shard_map/ppermute | solution.py:374
  57.0 8.3 %collective-permute-done.12 = bf16[432,384]{1,0:T(8,128)(2,1)} collective-permute-done((bf16[432,384]{1,0:T(8,128)(2,1)}, bf16[432,384]{1,0:T(8,128)(2,1)}, u32[]{:S(2)}, u32[]{:S(2)}) %collective-permute-start.12) | collective-permute-done | bytes 331808 | tf_op jit(solution)/shard_map/ppermute | solution.py:374
  70.8 2.9 collective-permute-start.11
  76.9 3.5 %shard_map.316 = (f32[3,8,512]{2,1,0:T(8,128)S(1)}, f32[3,8,512]{2,1,0:T(8,128)S(1)}, f32[192,512]{1,0:T(8,128)S(1)}) custom-call(bf16[192,512]{1,0:T(8,128)(2,1)S(1)} %fusion.15.refs_0_, bf16[384,512]{1,0:T(8,128)(2,1)S(1)} %fusion.9.refs_1_.refs_10_, bf16[384,512]{1,0:T(8,128)(2,1)S(1)} %collective-permute-done.15.refs_2_.refs_11_), custom_call_target="tpu_custom_call" | custom-call | flops 350000000 | bytes 350000 | tf_op jit(solution)/shard_map/pallas_call | solution.py:471
  80.8 4.0 %shard_map.315 = (bf16[192,512]{1,0:T(8,128)(2,1)S(1)}, f32[3,8,512]{2,1,0:T(8,128)S(1)}) custom-call(s32[1]{0:T(128)} %bitcast.25.refs_0_, bf16[192,512]{1,0:T(8,128)(2,1)S(1)} %fusion.14.refs_1_, bf16[384,512]{1,0:T(8,128)(2,1)S(1)} %fusion.10.refs_2_.refs_5_, bf16[384,512]{1,0:T(8,128)(2,1)S(1)} %collective-permute-done.17.refs_3_.refs_6_), custom_call_target="tpu_custom_call" | custom-call | flops 350000000 | bytes 350000 | tf_op jit(solution)/shard_map/pallas_call | solution.py:471
  84.9 5.6 %collective-permute-done.11.refs_1_.refs_6_ = bf16[384,512]{1,0:T(8,128)(2,1)S(1)} collective-permute-done((bf16[384,512]{1,0:T(8,128)(2,1)S(1)}, bf16[384,512]{1,0:T(8,128)(2,1)S(1)}, u32[]{:S(2)}, u32[]{:S(2)}) %collective-permute-start.11) | collective-permute-done | bytes 393248 | tf_op jit(solution)/shard_map/ppermute | solution.py:374
  94.7 3.5 %shard_map.317 = (f32[3,8,512]{2,1,0:T(8,128)S(1)}, f32[3,8,512]{2,1,0:T(8,128)S(1)}, f32[192,512]{1,0:T(8,128)S(1)}) custom-call(bf16[192,512]{1,0:T(8,128)(2,1)S(1)} %fusion.15.refs_0_, bf16[384,512]{1,0:T(8,128)(2,1)S(1)} %collective-permute-done.10.refs_1_.refs_8_, bf16[384,512]{1,0:T(8,128)(2,1)S(1)} %collective-permute-done.20.refs_2_.refs_9_, ...), custom_call_target="tpu_custom_call" | custom-call | flops 350000000 | bytes 350000 | tf_op jit(solution)/shard_map/pallas_call | solution.py:471
  98.3 3.5 %shard_map.318 = (f32[3,8,512]{2,1,0:T(8,128)S(1)}, f32[3,8,512]{2,1,0:T(8,128)S(1)}, f32[192,512]{1,0:T(8,128)S(1)}) custom-call(bf16[192,512]{1,0:T(8,128)(2,1)S(1)} %fusion.15.refs_0_, bf16[384,512]{1,0:T(8,128)(2,1)S(1)} %collective-permute-done.11.refs_1_.refs_6_, bf16[384,512]{1,0:T(8,128)(2,1)S(1)} %collective-permute-done.19.refs_2_.refs_7_, ...), custom_call_target="tpu_custom_call" | custom-call | flops 350000000 | bytes 350000 | tf_op jit(solution)/shard_map/pallas_call | solution.py:471
  103.9 3.5 %shard_map.319 = (bf16[192,512]{1,0:T(8,128)(2,1)S(1)}, f32[3,8,512]{2,1,0:T(8,128)S(1)}) custom-call(bf16[192,512]{1,0:T(8,128)(2,1)S(1)} %fusion.15.refs_0_, bf16[384,512]{1,0:T(8,128)(2,1)S(1)} %collective-permute-done.18.refs_1_.refs_4_, bf16[384,512]{1,0:T(8,128)(2,1)S(1)} %collective-permute-done.21.refs_2_.refs_5_, ...), custom_call_target="tpu_custom_call" | custom-call | flops 350000000 | bytes 350000 | tf_op jit(solution)/shard_map/pallas_call | solution.py:471
  109.4 5.1 %collective-permute-done.22.one_far = bf16[8,144,384]{2,1,0:T(8,128)(2,1)S(1)} collective-permute-done((bf16[8,144,384]{2,1,0:T(8,128)(2,1)S(1)}, bf16[8,144,384]{2,1,0:T(8,128)(2,1)S(1)}, u32[]{:S(2)}, u32[]{:S(2)}) %collective-permute-start.22) | collective-permute-done | bytes 884768 | tf_op jit(solution)/shard_map/ppermute | solution.py:386
  127.4 2.8 collective-permute-done.25
  137.0 9.7 %multiply_convert_fusion = (bf16[512,1536]{1,0:T(8,128)(2,1)S(1)}, f32[512,1536]{1,0:T(8,128)}, f32[512,1536]{1,0:T(8,128)}) fusion(f32[1536]{0:T(1024)S(1)} %slice_reduce_fusion, bf16[768,1536]{1,0:T(8,128)(2,1)S(1)} %bitcast.198, bf16[256,768]{1,0:T(8,128)(2,1)S(1)} %collective-permute-done.27, bf16[256,768]{1,0:T(8,128)(2,1)S(1)} %fusion.44), kind=kOutput, calls=%fused_computation.6 | convolution fusion | flops 1261436928 | bytes 11016192 | tf_op jit(solution)/shard_map/dot_general | solution.py:32
  146.8 4.7 %collective-permute-done.30.one_far = bf16[8,96,384]{2,1,0:T(8,128)(2,1)S(1)} collective-permute-done((bf16[8,96,384]{2,1,0:T(8,128)(2,1)S(1)}, bf16[8,96,384]{2,1,0:T(8,128)(2,1)S(1)}, u32[]{:S(2)}, u32[]{:S(2)}) %collective-permute-start.30) | collective-permute-done | bytes 589856 | tf_op jit(solution)/shard_map/ppermute | solution.py:386
  156.0 3.4 %fusion.89 = (f32[256]{0:T(256)S(1)}, f32[256,768]{1,0:T(8,128)S(1)}, f32[256,768]{1,0:T(8,128)}) fusion(f32[768]{0:T(1024)} %copy-done.94, f32[768]{0:T(1024)S(1)} %get-tuple-element.254, f32[256]{0:T(256)} %copy-done.95, f32[256,768]{1,0:T(8,128)} %copy-done.44, f32[256]{0:T(256)} %copy-done.88, f32[768]{0:T(1024)} %get-tuple-element.252, ...), kind=kOutput, calls=%fused_computation.272 | convolution fusion | flops 605748992 | bytes 5912576 | tf_op jit(solution)/shard_map/dot_general | solution.py:32
  164.3 2.9 convert_reduce_fusion
  181.9 5.7 %collective-permute-done.37 = bf16[384,256]{1,0:T(8,128)(2,1)S(1)} collective-permute-done((bf16[384,256]{1,0:T(8,128)(2,1)S(1)}, bf16[384,256]{1,0:T(8,128)(2,1)S(1)}, u32[]{:S(2)}, u32[]{:S(2)}) %collective-permute-start.37) | collective-permute-done | bytes 196640 | tf_op jit(solution)/shard_map/ppermute | solution.py:374
  200.7 20.2 %shard_map.322 = (f32[192,512]{1,0:T(8,128)S(1)}, bf16[384,512]{1,0:T(8,128)(2,1)S(1)}, bf16[384,512]{1,0:T(8,128)(2,1)S(1)}, bf16[384,512]{1,0:T(8,128)(2,1)S(1...) custom-call(bf16[192,512]{1,0:T(8,128)(2,1)S(1)} %fusion.15.refs_0_,, ...), custom_call_target="tpu_custom_call" | custom-call | flops 1000000000 | bytes 1000000 | tf_op jit(solution)/shard_map/pallas_call | solution.py:544
  223.6 5.7 %shard_map.323 = (f32[192,512]{1,0:T(8,128)S(1)}, bf16[384,512]{1,0:T(8,128)(2,1)S(1)}, bf16[384,512]{1,0:T(8,128)(2,1)S(1)}) custom-call(s32[1]{0:T(128)} %bitcast.25.refs_0_, bf16[192,512]{1,0:T(8,128)(2,1)S(1)} %copy-done.41, bf16[192,512]{1,0:T(8,128)(2,1)S(1)} %pad_maximum_fusion.29.refs_2_, f32[3,8,512]{2,1,0:T(8,128)S(1)} %copy-done.43, ...), custom_call_target="tpu_custom_call" | custom-call | flops 1000000000 | bytes 1000000 | tf_op jit(solution)/shard_map/pallas_call | solution.py:544
  231.5 2.1 collective-permute-start.46
  238.0 5.3 %collective-permute-done.44 = bf16[384,512]{1,0:T(8,128)(2,1)S(1)} collective-permute-done((bf16[384,512]{1,0:T(8,128)(2,1)S(1)}, bf16[384,512]{1,0:T(8,128)(2,1)S(1)}, u32[]{:S(2)}, u32[]{:S(2)}) %collective-permute-start.44) | collective-permute-done | bytes 393248 | tf_op jit(solution)/shard_map/ppermute | solution.py:374
  246.8 4.5 %collective-permute-done.48 = bf16[4,192,384]{2,1,0:T(8,128)(2,1)S(1)} collective-permute-done((bf16[4,192,384]{2,1,0:T(8,128)(2,1)S(1)}, bf16[4,192,384]{2,1,0:T(8,128)(2,1)S(1)}, u32[]{:S(2)}, u32[]{:S(2)}) %collective-permute-start.48) | collective-permute-done | bytes 589856 | tf_op jit(solution)/shard_map/ppermute | solution.py:386
  251.5 4.0 %collective-permute-done.47 = bf16[4,240,384]{2,1,0:T(8,128)(2,1)S(1)} collective-permute-done((bf16[4,240,384]{2,1,0:T(8,128)(2,1)S(1)}, bf16[4,240,384]{2,1,0:T(8,128)(2,1)S(1)}, u32[]{:S(2)}, u32[]{:S(2)}) %collective-permute-start.47) | collective-permute-done | bytes 737312 | tf_op jit(solution)/shard_map/ppermute | solution.py:374
  275.2 15.3 %collective-permute-done.59 = bf16[432,384]{1,0:T(8,128)(2,1)S(1)} collective-permute-done((bf16[432,384]{1,0:T(8,128)(2,1)S(1)}, bf16[432,384]{1,0:T(8,128)(2,1)S(1)}, u32[]{:S(2)}, u32[]{:S(2)}) %collective-permute-start.59) | collective-permute-done | bytes 331808 | tf_op jit(solution)/shard_map/ppermute | solution.py:374
  291.0 2.7 collective-permute-done.56
  295.6 6.5 %collective-permute-done.55 = bf16[2,56,576]{2,1,0:T(8,128)(2,1)S(1)} collective-permute-done((bf16[2,56,576]{2,1,0:T(8,128)(2,1)S(1)}, bf16[2,56,576]{2,1,0:T(8,128)(2,1)S(1)}, u32[]{:S(2)}, u32[]{:S(2)}) %collective-permute-start.55) | collective-permute-done | bytes 129056 | tf_op jit(solution)/shard_map/ppermute | solution.py:374
  302.0 11.2 %collective-permute-done.57 = bf16[2,56,576]{2,1,0:T(8,128)(2,1)S(1)} collective-permute-done((bf16[2,56,576]{2,1,0:T(8,128)(2,1)S(1)}, bf16[2,56,576]{2,1,0:T(8,128)(2,1)S(1)}, u32[]{:S(2)}, u32[]{:S(2)}) %collective-permute-start.57) | collective-permute-done | bytes 129056 | tf_op jit(solution)/shard_map/ppermute | solution.py:374
  315.0 2.7 collective-permute-done.61
  (481 shorter events, 138.0 us)
Async XLA Ops:
  7.1 12.3 %collective-permute-start.3 = (bf16[256,768]{1,0:T(8,128)(2,1)S(1)}, bf16[256,768]{1,0:T(8,128)(2,1)S(1)}, u32[]{:S(2)}, u32[]{:S(2)}) collective-permute-start(bf16[256,768]{1,0:T(8,128)(2,1)S(1)} %bitcast.210), channel_id=1, source_target_pairs={{0,1},{1,0},{2,3},{3,2},{4,5},{5,4},{6,7},{7,6},{8,9},{9,8},{10,11... | collective-permute-start | bytes 1179656 | tf_op jit(solution)/shard_map/ppermute | solution.py:386
  19.7 24.8 %collective-permute-start.6 = (bf16[256,768]{1,0:T(8,128)(2,1)S(1)}, bf16[256,768]{1,0:T(8,128)(2,1)S(1)}, u32[]{:S(2)}, u32[]{:S(2)}) collective-permute-start(bf16[256,768]{1,0:T(8,128)(2,1)S(1)} %get-tuple-element.136), channel_id=1, source_target_pairs={{0,4},{2,6},{4,0},{6,2},{8,12},{10,14},{12,8},{14,10},{16,20},{18,... | collective-permute-start | bytes 1179656 | tf_op jit(solution)/shard_map/ppermute | solution.py:374
  21.3 23.9 %collective-permute-start.8 = (bf16[432,384]{1,0:T(8,128)(2,1)S(1)}, bf16[432,384]{1,0:T(8,128)(2,1)}, u32[]{:S(2)}, u32[]{:S(2)}) collective-permute-start(bf16[432,384]{1,0:T(8,128)(2,1)S(1)} %fusion.58), channel_id=1, source_target_pairs={{0,16},{2,18},{4,20},{6,22},{8,24},{10,26},{12,28},{14,30},{16,0},... | collective-permute-start | bytes 995336 | tf_op jit(solution)/shard_map/ppermute | solution.py:374
  25.6 19.0 %collective-permute-start.5 = (bf16[2,56,576]{2,1,0:T(8,128)(2,1)S(1)}, bf16[2,56,576]{2,1,0:T(8,128)(2,1)S(1)}, u32[]{:S(2)}, u32[]{:S(2)}) collective-permute-start(bf16[2,56,576]{2,1,0:T(8,128)(2,1)S(1)} %get-tuple-element.328), channel_id=1, source_target_pairs={{0,16},{2,18},{4,20},{6,22},{8,24},{10,26},{12,28},{14,30},{16,0},... | collective-permute-start | bytes 387080 | tf_op jit(solution)/shard_map/ppermute | solution.py:374
  56.5 19.0 %collective-permute-start.16 = (bf16[256,768]{1,0:T(8,128)(2,1)S(1)}, bf16[256,768]{1,0:T(8,128)(2,1)S(1)}, u32[]{:S(2)}, u32[]{:S(2)}) collective-permute-start(bf16[256,768]{1,0:T(8,128)(2,1)S(1)} %get-tuple-element.147), channel_id=1, source_target_pairs={{0,4},{2,6},{4,0},{6,2},{8,12},{10,14},{12,8},{14,10},{16,20},{18,... | collective-permute-start | bytes 1179656 | tf_op jit(solution)/shard_map/ppermute | solution.py:374
  68.7 16.1 %collective-permute-start.14 = (bf16[4,96,384]{2,1,0:T(8,128)(2,1)S(1)}, bf16[4,96,384]{2,1,0:T(8,128)(2,1)S(1)}, u32[]{:S(2)}, u32[]{:S(2)}) collective-permute-start(bf16[4,96,384]{2,1,0:T(8,128)(2,1)S(1)} %get-tuple-element.277), channel_id=1, source_target_pairs={{0,1},{1,0},{2,3},{3,2},{4,5},{5,4},{6,7},{7,6},{8,9},{9,8},{10,11... | collective-permute-start | bytes 884744 | tf_op jit(solution)/shard_map/ppermute | solution.py:386
  70.2 14.7 %collective-permute-start.13 = (bf16[4,144,384]{2,1,0:T(8,128)(2,1)S(1)}, bf16[4,144,384]{2,1,0:T(8,128)(2,1)S(1)}, u32[]{:S(2)}, u32[]{:S(2)}) collective-permute-start(bf16[4,144,384]{2,1,0:T(8,128)(2,1)S(1)} %slice.428), channel_id=1, source_target_pairs={{0,4},{2,6},{4,0},{6,2},{8,12},{10,14},{12,8},{14,10},{16,20},{18,... | collective-permute-start | bytes 1327112 | tf_op jit(solution)/shard_map/ppermute | solution.py:374
  70.8 19.7 %collective-permute-start.11 = (bf16[384,512]{1,0:T(8,128)(2,1)S(1)}, bf16[384,512]{1,0:T(8,128)(2,1)S(1)}, u32[]{:S(2)}, u32[]{:S(2)}) collective-permute-start(bf16[384,512]{1,0:T(8,128)(2,1)S(1)} %fusion.9.refs_1_.refs_10_), channel_id=1, source_target_pairs={{0,16},{2,18},{4,20},{6,22},{8,24},{10,26},{12,28},{14,30},{16,0},... | collective-permute-start | bytes 1179656 | tf_op jit(solution)/shard_map/ppermute | solution.py:374
  73.7 16.9 %collective-permute-start.10 = (bf16[384,512]{1,0:T(8,128)(2,1)S(1)}, bf16[384,512]{1,0:T(8,128)(2,1)S(1)}, u32[]{:S(2)}, u32[]{:S(2)}) collective-permute-start(bf16[384,512]{1,0:T(8,128)(2,1)S(1)} %fusion.9.refs_1_.refs_10_), channel_id=1, source_target_pairs={{0,8},{2,10},{4,12},{6,14},{8,0},{10,2},{12,4},{14,6},{16,24},{18,... | collective-permute-start | bytes 1179656 | tf_op jit(solution)/shard_map/ppermute | solution.py:374
  90.6 11.5 %collective-permute-start.18 = (bf16[384,512]{1,0:T(8,128)(2,1)S(1)}, bf16[384,512]{1,0:T(8,128)(2,1)S(1)}, u32[]{:S(2)}, u32[]{:S(2)}) collective-permute-start(bf16[384,512]{1,0:T(8,128)(2,1)S(1)} %collective-permute-done.11.refs_1_.refs_6_), channel_id=1, source_target_pairs={{0,8},{2,10},{4,12},{6,14},{8,0},{10,2},{12,4},{14,6},{16,24},{18,... | collective-permute-start | bytes 1179656 | tf_op jit(solution)/shard_map/ppermute | solution.py:374
  92.5 22.0 %collective-permute-start.22 = (bf16[8,144,384]{2,1,0:T(8,128)(2,1)S(1)}, bf16[8,144,384]{2,1,0:T(8,128)(2,1)S(1)}, u32[]{:S(2)}, u32[]{:S(2)}) collective-permute-start(bf16[8,144,384]{2,1,0:T(8,128)(2,1)S(1)} %pad_maximum_fusion.4.one_own), channel_id=1, source_target_pairs={{0,1},{1,0},{2,3},{3,2},{4,5},{5,4},{6,7},{7,6},{8,9},{9,8},{10,11... | collective-permute-start | bytes 2654216 | tf_op jit(solution)/shard_map/ppermute | solution.py:386
  93.2 15.4 %collective-permute-start.23 = (bf16[2,4,96,384]{3,2,1,0:T(8,128)(2,1)S(1)}, bf16[2,4,96,384]{3,2,1,0:T(8,128)(2,1)S(1)}, u32[]{:S(2)}, u32[]{:S(2)}) collective-permute-start(bf16[2,4,96,384]{3,2,1,0:T(8,128)(2,1)S(1)} %pad_maximum_fusion.7.two_own), channel_id=1, source_target_pairs={{0,4},{2,6},{4,0},{6,2},{8,12},{10,14},{12,8},{14,10},{16,20},{18,... | collective-permute-start | bytes 1769480 | tf_op jit(solution)/shard_map/ppermute | solution.py:374
  124.5 11.7 %collective-permute-start.28 = (bf16[4,96,384]{2,1,0:T(8,128)(2,1)}, bf16[4,96,384]{2,1,0:T(8,128)(2,1)S(1)}, u32[]{:S(2)}, u32[]{:S(2)}) collective-permute-start(bf16[4,96,384]{2,1,0:T(8,128)(2,1)} %get-tuple-element.179), channel_id=1, source_target_pairs={{0,4},{2,6},{4,0},{6,2},{8,12},{10,14},{12,8},{14,10},{16,20},{18,... | collective-permute-start | bytes 884744 | tf_op jit(solution)/shard_map/ppermute | solution.py:374
  136.3 15.2 %collective-permute-start.30 = (bf16[8,96,384]{2,1,0:T(8,128)(2,1)S(1)}, bf16[8,96,384]{2,1,0:T(8,128)(2,1)S(1)}, u32[]{:S(2)}, u32[]{:S(2)}) collective-permute-start(bf16[8,96,384]{2,1,0:T(8,128)(2,1)S(1)} %constant_dynamic-update-slice_fusion.4.one_own), channel_id=1, source_target_pairs={{0,1},{1,0},{2,3},{3,2},{4,5},{5,4},{6,7},{7,6},{8,9},{9,8},{10,11... | collective-permute-start | bytes 1769480 | tf_op jit(solution)/shard_map/ppermute | solution.py:386
  136.4 15.2 %collective-permute-start.31 = (bf16[2,4,96,384]{3,2,1,0:T(8,128)(2,1)S(1)}, bf16[2,4,96,384]{3,2,1,0:T(8,128)(2,1)S(1)}, u32[]{:S(2)}, u32[]{:S(2)}) collective-permute-start(bf16[2,4,96,384]{3,2,1,0:T(8,128)(2,1)S(1)} %pad_maximum_fusion.8.two_own), channel_id=1, source_target_pairs={{0,4},{2,6},{4,0},{6,2},{8,12},{10,14},{12,8},{14,10},{16,20},{18,... | collective-permute-start | bytes 1769480 | tf_op jit(solution)/shard_map/ppermute | solution.py:374
  175.8 13.1 %collective-permute-start.35 = (bf16[4,2,48,768]{3,2,0,1:T(8,128)(2,1)S(1)}, bf16[4,2,48,768]{3,2,0,1:T(8,128)(2,1)S(1)}, u32[]{:S(2)}, u32[]{:S(2)}) collective-permute-start(bf16[4,2,48,768]{3,2,0,1:T(8,128)(2,1)S(1)} %select_bitcast_fusion.2), channel_id=1, source_target_pairs={{0,2},{2,0},{4,6},{6,4},{8,10},{10,8},{12,14},{14,12},{16,18},{18,... | collective-permute-start | bytes 1769480 | tf_op jit(solution)/shard_map/ppermute | solution.py:374
  191.3 37.9 %collective-permute-start.42 = (bf16[4,2,240,384]{3,2,0,1:T(8,128)(2,1)}, bf16[4,2,240,384]{3,2,0,1:T(8,128)(2,1)}, u32[]{:S(2)}, u32[]{:S(2)}) collective-permute-start(bf16[4,2,240,384]{3,2,0,1:T(8,128)(2,1)} %pad_maximum_fusion), channel_id=1, source_target_pairs={{0,1},{1,0},{2,3},{3,2},{4,5},{5,4},{6,7},{7,6},{8,9},{9,8},{10,11... | collective-permute-start | bytes 4423688 | tf_op jit(solution)/shard_map/ppermute | solution.py:386
  192.8 36.5 %collective-permute-start.43 = (bf16[4,192,768]{2,1,0:T(8,128)(2,1)}, bf16[4,192,768]{2,1,0:T(8,128)(2,1)}, u32[]{:S(2)}, u32[]{:S(2)}) collective-permute-start(bf16[4,192,768]{2,1,0:T(8,128)(2,1)} %select_bitcast_fusion), channel_id=1, source_target_pairs={{0,4},{2,6},{4,0},{6,2},{8,12},{10,14},{12,8},{14,10},{16,20},{18,... | collective-permute-start | bytes 3538952 | tf_op jit(solution)/shard_map/ppermute | solution.py:374
  231.3 12.0 %collective-permute-start.44 = (bf16[384,512]{1,0:T(8,128)(2,1)S(1)}, bf16[384,512]{1,0:T(8,128)(2,1)S(1)}, u32[]{:S(2)}, u32[]{:S(2)}) collective-permute-start(bf16[384,512]{1,0:T(8,128)(2,1)S(1)} %add_convert_fusion.9), channel_id=1, source_target_pairs={{0,8},{2,10},{4,12},{6,14},{8,0},{10,2},{12,4},{14,6},{16,24},{18,... | collective-permute-start | bytes 1179656 | tf_op jit(solution)/shard_map/ppermute | solution.py:374
  231.5 31.0 %collective-permute-start.46 = (bf16[384,512]{1,0:T(8,128)(2,1)S(1)}, bf16[384,512]{1,0:T(8,128)(2,1)S(1)}, u32[]{:S(2)}, u32[]{:S(2)}) collective-permute-start(bf16[384,512]{1,0:T(8,128)(2,1)S(1)} %add_convert_fusion.7), channel_id=1, source_target_pairs={{0,8},{2,10},{4,12},{6,14},{8,0},{10,2},{12,4},{14,6},{16,24},{18,... | collective-permute-start | bytes 1179656 | tf_op jit(solution)/shard_map/ppermute | solution.py:374
  235.5 15.7 %collective-permute-start.48 = (bf16[4,192,384]{2,1,0:T(8,128)(2,1)S(1)}, bf16[4,192,384]{2,1,0:T(8,128)(2,1)S(1)}, u32[]{:S(2)}, u32[]{:S(2)}) collective-permute-start(bf16[4,192,384]{2,1,0:T(8,128)(2,1)S(1)} %broadcast_select_fusion), channel_id=1, source_target_pairs={{0,1},{1,0},{2,3},{3,2},{4,5},{5,4},{6,7},{7,6},{8,9},{9,8},{10,11... | collective-permute-start | bytes 1769480 | tf_op jit(solution)/shard_map/ppermute | solution.py:386
  236.2 19.3 %collective-permute-start.47 = (bf16[4,240,384]{2,1,0:T(8,128)(2,1)S(1)}, bf16[4,240,384]{2,1,0:T(8,128)(2,1)S(1)}, u32[]{:S(2)}, u32[]{:S(2)}) collective-permute-start(bf16[4,240,384]{2,1,0:T(8,128)(2,1)S(1)} %select_bitcast_fusion.1), channel_id=1, source_target_pairs={{0,4},{2,6},{4,0},{6,2},{8,12},{10,14},{12,8},{14,10},{16,20},{18,... | collective-permute-start | bytes 2211848 | tf_op jit(solution)/shard_map/ppermute | solution.py:374
  243.4 19.1 %collective-permute-start.45 = (bf16[384,512]{1,0:T(8,128)(2,1)S(1)}, bf16[384,512]{1,0:T(8,128)(2,1)S(1)}, u32[]{:S(2)}, u32[]{:S(2)}) collective-permute-start(bf16[384,512]{1,0:T(8,128)(2,1)S(1)} %add_convert_fusion.8), channel_id=1, source_target_pairs={{0,16},{2,18},{4,20},{6,22},{8,24},{10,26},{12,28},{14,30},{16,0},... | collective-permute-start | bytes 1179656 | tf_op jit(solution)/shard_map/ppermute | solution.py:374
  244.5 18.6 %collective-permute-start.51 = (bf16[256,768]{1,0:T(8,128)(2,1)S(1)}, bf16[256,768]{1,0:T(8,128)(2,1)S(1)}, u32[]{:S(2)}, u32[]{:S(2)}) collective-permute-start(bf16[256,768]{1,0:T(8,128)(2,1)S(1)} %slice.676), channel_id=1, source_target_pairs={{0,4},{2,6},{4,0},{6,2},{8,12},{10,14},{12,8},{14,10},{16,20},{18,... | collective-permute-start | bytes 1179656 | tf_op jit(solution)/shard_map/ppermute | solution.py:374
  270.0 23.9 %collective-permute-start.52 = (bf16[256,768]{1,0:T(8,128)(2,1)S(1)}, bf16[256,768]{1,0:T(8,128)(2,1)S(1)}, u32[]{:S(2)}, u32[]{:S(2)}) collective-permute-start(bf16[256,768]{1,0:T(8,128)(2,1)S(1)} %slice.675), channel_id=1, source_target_pairs={{0,4},{2,6},{4,0},{6,2},{8,12},{10,14},{12,8},{14,10},{16,20},{18,... | collective-permute-start | bytes 1179656 | tf_op jit(solution)/shard_map/ppermute | solution.py:374
  272.7 42.3 %collective-permute-start.58 = (bf16[432,384]{1,0:T(8,128)(2,1)S(1)}, bf16[432,384]{1,0:T(8,128)(2,1)S(1)}, u32[]{:S(2)}, u32[]{:S(2)}) collective-permute-start(bf16[432,384]{1,0:T(8,128)(2,1)S(1)} %get-tuple-element.276), channel_id=1, source_target_pairs={{0,8},{2,10},{4,12},{6,14},{8,0},{10,2},{12,4},{14,6},{16,24},{18,... | collective-permute-start | bytes 995336 | tf_op jit(solution)/shard_map/ppermute | solution.py:374
  272.8 17.7 %collective-permute-start.59 = (bf16[432,384]{1,0:T(8,128)(2,1)S(1)}, bf16[432,384]{1,0:T(8,128)(2,1)S(1)}, u32[]{:S(2)}, u32[]{:S(2)}) collective-permute-start(bf16[432,384]{1,0:T(8,128)(2,1)S(1)} %get-tuple-element.275), channel_id=1, source_target_pairs={{0,8},{2,10},{4,12},{6,14},{8,0},{10,2},{12,4},{14,6},{16,24},{18,... | collective-permute-start | bytes 995336 | tf_op jit(solution)/shard_map/ppermute | solution.py:374
  275.1 18.6 %collective-permute-start.56 = (bf16[2,56,576]{2,1,0:T(8,128)(2,1)S(1)}, bf16[2,56,576]{2,1,0:T(8,128)(2,1)S(1)}, u32[]{:S(2)}, u32[]{:S(2)}) collective-permute-start(bf16[2,56,576]{2,1,0:T(8,128)(2,1)S(1)} %get-tuple-element.298), channel_id=1, source_target_pairs={{0,8},{2,10},{4,12},{6,14},{8,0},{10,2},{12,4},{14,6},{16,24},{18,... | collective-permute-start | bytes 387080 | tf_op jit(solution)/shard_map/ppermute | solution.py:374
  290.6 24.4 %collective-permute-start.60 = (bf16[432,384]{1,0:T(8,128)(2,1)S(1)}, bf16[432,384]{1,0:T(8,128)(2,1)S(1)}, u32[]{:S(2)}, u32[]{:S(2)}) collective-permute-start(bf16[432,384]{1,0:T(8,128)(2,1)S(1)} %fusion.42), channel_id=1, source_target_pairs={{0,16},{2,18},{4,20},{6,22},{8,24},{10,26},{12,28},{14,30},{16,0},... | collective-permute-start | bytes 995336 | tf_op jit(solution)/shard_map/ppermute | solution.py:374
  290.7 11.4 %collective-permute-start.55 = (bf16[2,56,576]{2,1,0:T(8,128)(2,1)S(1)}, bf16[2,56,576]{2,1,0:T(8,128)(2,1)S(1)}, u32[]{:S(2)}, u32[]{:S(2)}) collective-permute-start(bf16[2,56,576]{2,1,0:T(8,128)(2,1)S(1)} %get-tuple-element.297), channel_id=1, source_target_pairs={{0,8},{2,10},{4,12},{6,14},{8,0},{10,2},{12,4},{14,6},{16,24},{18,... | collective-permute-start | bytes 387080 | tf_op jit(solution)/shard_map/ppermute | solution.py:374
  293.7 19.5 %collective-permute-start.57 = (bf16[2,56,576]{2,1,0:T(8,128)(2,1)S(1)}, bf16[2,56,576]{2,1,0:T(8,128)(2,1)S(1)}, u32[]{:S(2)}, u32[]{:S(2)}) collective-permute-start(bf16[2,56,576]{2,1,0:T(8,128)(2,1)S(1)} %fusion.59), channel_id=1, source_target_pairs={{0,16},{2,18},{4,20},{6,22},{8,24},{10,26},{12,28},{14,30},{16,0},... | collective-permute-start | bytes 387080 | tf_op jit(solution)/shard_map/ppermute | solution.py:374
  294.1 19.9 %collective-permute-start.53 = (bf16[256,768]{1,0:T(8,128)(2,1)S(1)}, bf16[256,768]{1,0:T(8,128)(2,1)S(1)}, u32[]{:S(2)}, u32[]{:S(2)}) collective-permute-start(bf16[256,768]{1,0:T(8,128)(2,1)S(1)} %select_convert_fusion), channel_id=1, source_target_pairs={{0,1},{1,0},{2,3},{3,2},{4,5},{5,4},{6,7},{7,6},{8,9},{9,8},{10,11... | collective-permute-start | bytes 1179656 | tf_op jit(solution)/shard_map/ppermute | solution.py:386
  (140 other events, 880.9 us)
where the time goes:
time: 332 us; the launch traced here: 326 us
  waiting for transfers between devices  127 us (38%)
  starting transfers between devices  51.5 us (16%)
  Pallas kernels  49 us (15%)
  matrix products  32.4 us (10%)
  other arithmetic  31.9 us (10%)
  local copies, waits for them, and re-layouts  29.4 us (9%)
  between operations  4.9 us (1%)
    ppermute x52, waiting for transfers between devices, ctx_move(): return lax.ppermute(value, 'ctx', [(i, i ^ mask) for i in range(16)])  102 us
    ppermute x52, starting transfers between devices, ctx_move(): return lax.ppermute(value, 'ctx', [(i, i ^ mask) for i in range(16)])  37.8 us
    pallas_call x2, Pallas kernels, attend_back_call(): pl.pallas_call(functools.partial(attend_back_kernel, len(pairs), grad_que...  25.9 us
    ppermute x11, waiting for transfers between devices, x_swap(): return lax.ppermute(value, 'fsdp', [(0, 1), (1, 0)])  25.2 us
    pallas_call x5, Pallas kernels, attend_call(): pl.pallas_call(functools.partial(attend_kernel, len(pairs), state is None...  18 us
    dot_general x4, matrix products, plain_product(): return jnp.dot(left_side, right_side, preferred_element_type=jnp.float32)  15.1 us
    unnamed x221, local copies, waits for them, and re-layouts  14.9 us
    ppermute x11, starting transfers between devices, x_swap(): return lax.ppermute(value, 'fsdp', [(0, 1), (1, 0)])  13.7 us
  transfers between devices with their start and end apart: 63, of which 34 were waited for; matrix products, arithmetic and copies ran while one was open for 14% of the time, Pallas kernels for 14%

commit v1 on v0

--- a/solution.py
+++ b/solution.py
@@ -773,10 +773,11 @@
         return query.astype(jnp.bfloat16) * scale, pair.astype(jnp.bfloat16)
 
     long_query, long_pair = project(long_rows)
+    short_own, _ = hold(short_own, z_three)
+    short_far = y_swap(short_own)
+    long_pair, ffn_three, short_far = hold(long_pair, ffn_three, short_far)
     kv_two, kv_one = ctx_move(long_pair, 8), ctx_move(long_pair, 4)
     long_pair_far = core_swap(long_pair)
-    short_own, long_pair_far = hold(short_own, long_pair_far)
-    short_far = y_swap(short_own)
     state = attend_call(long_query, (long_pair, long_pair_far))
     short_rows = jnp.concatenate([short_own, short_far], axis=0)
     short_query, short_pair = project(short_rows)
@@ -1011,9 +1012,20 @@
     in_sum = add_b(jnp.where(y_low, in_sum[:, 0], in_sum[:, 1]), in_y)
     down_sum = add_b(jnp.where(x_low, down_sum[..., :384], down_sum[..., 384:]), down_x)
     ffn_sum = jnp.concatenate([in_sum, down_sum], axis=1)
-    two_got, one_got, ffn_sum, owner_sums, short_got, short_rows_back = hold(
-        two_got, one_got, ffn_sum, owner_sums, short_got, short_rows_back
-    )
+    def by_z(stack):
+        return [
+            lax.dynamic_index_in_dim(stack, z_at ^ mask, 0, keepdims=False) for mask in range(4)
+        ]
+
+    ffn_own, ffn_first, ffn_second, ffn_third = by_z(ffn_sum)
+    ffn_third = ctx_move(ffn_third, 4)
+    two_got, one_got, ffn_own, ffn_first, ffn_second, ffn_third = hold(
+        two_got, one_got, ffn_own, ffn_first, ffn_second, ffn_third
+    )
+    two_got, owner_sums, short_got, short_rows_back = hold(
+        two_got, owner_sums, short_got, short_rows_back
+    )
+    ffn_second = add_b(ffn_second, ffn_third)
     long_pair_grad = near_own.astype(jnp.float32)
     for got_part in (far_own, one_got, two_got):
         long_pair_grad = long_pair_grad + got_part.astype(jnp.float32)
@@ -1032,11 +1044,6 @@
     core_send = jnp.where(core_low, grad_qkv[:, :, 1], grad_qkv[:, :, 0])
     core_sum = add_b(core_keep, core_swap(core_send))
 
-    def by_z(stack):
-        return [
-            lax.dynamic_index_in_dim(stack, z_at ^ mask, 0, keepdims=False) for mask in range(4)
-        ]
-
     own_sum, one_part, two_part, three_part = by_z(core_sum)
     one_part, three_part = ctx_move(one_part, 4), ctx_move(three_part, 4)
     two_part, qkv_hop = hold(add_b(two_part, three_part), three_part)
@@ -1044,11 +1051,10 @@
     own_sum = sum(part.astype(jnp.float32) for part in (own_sum, one_part, two_part))
     y_keep = jnp.where(y_low, own_sum[0], own_sum[1])
     y_got = y_swap(jnp.where(y_low, own_sum[1], own_sum[0]).astype(jnp.bfloat16))
-    own_part, one_part, two_part, three_part = by_z(ffn_sum)
-    one_part, _ = hold(one_part, qkv_hop)
-    one_part = ctx_move(one_part, 4)
-    two_part = ctx_move(add_b(two_part, ctx_move(three_part, 4)), 8)
-    one_part, two_part, y_got = hold(one_part, two_part, y_got)
+    own_part = ffn_own
+    ffn_first, _ = hold(ffn_first, qkv_hop)
+    one_part, two_part = ctx_move(ffn_first, 4), ctx_move(ffn_second, 8)
+    one_part, two_part, y_keep = hold(one_part, two_part, y_keep)
     ffn_owned = sum(part.astype(jnp.float32) for part in (own_part, one_part, two_part))
     y_got = y_got.astype(jnp.float32)
     vector_sums = y_keep[48:] + y_got[48:]

time: 332 us -> 316 us (0.952)
  waiting for transfers between devices: 127 us -> 118 us
  starting transfers between devices: 51.5 us -> 48.1 us
    ppermute x52, waiting for transfers between devices: 102 us -> 94.3 us  [ctx_move(): return lax.ppermute(value, 'ctx', [(i, i ^ mask) for i in range(16)])]
    ppermute x52, starting transfers between devices: 37.8 us -> 33.3 us  [ctx_move(): return lax.ppermute(value, 'ctx', [(i, i ^ mask) for i in range(16)])]
    unnamed x221 -> x227, local copies, waits for them, and re-layouts: 14.9 us -> 14.3 us
  transfers between devices with their start and end apart: 63 -> 63, of which waited for: 34 -> 32; matrix products, arithmetic and copies ran while one was open for 14% -> 16% of each run, Pallas kernels for 14% -> 15%
where the time goes in v1:
time: 316 us; the launch traced here: 310 us
  waiting for transfers between devices  118 us (37%)
  Pallas kernels  49.2 us (16%)
  starting transfers between devices  48.1 us (15%)
  matrix products  32.4 us (10%)
  local copies, waits for them, and re-layouts  28.7 us (9%)
  other arithmetic  28.6 us (9%)
  between operations  4.93 us (2%)
    ppermute x52, waiting for transfers between devices, ctx_move(): return lax.ppermute(value, 'ctx', [(i, i ^ mask) for i in range(16)])  94.3 us
    ppermute x52, starting transfers between devices, ctx_move(): return lax.ppermute(value, 'ctx', [(i, i ^ mask) for i in range(16)])  33.3 us
    pallas_call x2, Pallas kernels, attend_back_call(): pl.pallas_call(functools.partial(attend_back_kernel, len(pairs), grad_que...  26 us
    ppermute x11, waiting for transfers between devices, x_swap(): return lax.ppermute(value, 'fsdp', [(0, 1), (1, 0)])  24.2 us
    pallas_call x5, Pallas kernels, attend_call(): pl.pallas_call(functools.partial(attend_kernel, len(pairs), state is None...  18.1 us
    dot_general x4, matrix products, plain_product(): return jnp.dot(left_side, right_side, preferred_element_type=jnp.float32)  15.1 us
    ppermute x11, starting transfers between devices, x_swap(): return lax.ppermute(value, 'fsdp', [(0, 1), (1, 0)])  14.8 us
    unnamed x227, local copies, waits for them, and re-layouts  14.3 us
  transfers between devices with their start and end apart: 63, of which 32 were waited for; matrix products, arithmetic and copies ran while one was open for 16% of the time, Pallas kernels for 15%

profile of v1, /device:TPU:0, one launch (start us, length us, event | category | flops | bytes accessed | tf_op | source)
XLA Modules:
  0.0 310.4 jit_solution(15275984358665079427)
XLA Ops:
  7.1 2.6 collective-permute-start.3
  13.6 5.8 %collective-permute-done.3 = bf16[256,768]{1,0:T(8,128)(2,1)S(1)} collective-permute-done((bf16[256,768]{1,0:T(8,128)(2,1)S(1)}, bf16[256,768]{1,0:T(8,128)(2,1)S(1)}, u32[]{:S(2)}, u32[]{:S(2)}) %collective-permute-start.3) | collective-permute-done | bytes 393248 | tf_op jit(solution)/shard_map/ppermute | solution.py:386
  21.3 2.6 collective-permute-start.8
  25.9 9.2 %collective-permute-done.4 = bf16[2,56,576]{2,1,0:T(8,128)(2,1)S(1)} collective-permute-done((bf16[2,56,576]{2,1,0:T(8,128)(2,1)S(1)}, bf16[2,56,576]{2,1,0:T(8,128)(2,1)S(1)}, u32[]{:S(2)}, u32[]{:S(2)}) %collective-permute-start.4) | collective-permute-done | bytes 129056 | tf_op jit(solution)/shard_map/ppermute | solution.py:374
  35.1 9.4 %collective-permute-done.5 = bf16[2,56,576]{2,1,0:T(8,128)(2,1)S(1)} collective-permute-done((bf16[2,56,576]{2,1,0:T(8,128)(2,1)S(1)}, bf16[2,56,576]{2,1,0:T(8,128)(2,1)S(1)}, u32[]{:S(2)}, u32[]{:S(2)}) %collective-permute-start.5) | collective-permute-done | bytes 129056 | tf_op jit(solution)/shard_map/ppermute | solution.py:374
  45.2 4.4 %collective-permute-done.7 = bf16[2,56,576]{2,1,0:T(8,128)(2,1)S(1)} collective-permute-done((bf16[2,56,576]{2,1,0:T(8,128)(2,1)S(1)}, bf16[2,56,576]{2,1,0:T(8,128)(2,1)S(1)}, u32[]{:S(2)}, u32[]{:S(2)}) %collective-permute-start.7) | collective-permute-done | bytes 129056 | tf_op jit(solution)/shard_map/ppermute | solution.py:374
  54.5 6.7 %collective-permute-done.10 = bf16[432,384]{1,0:T(8,128)(2,1)S(1)} collective-permute-done((bf16[432,384]{1,0:T(8,128)(2,1)S(1)}, bf16[432,384]{1,0:T(8,128)(2,1)S(1)}, u32[]{:S(2)}, u32[]{:S(2)}) %collective-permute-start.10) | collective-permute-done | bytes 331808 | tf_op jit(solution)/shard_map/ppermute | solution.py:374
  61.2 2.3 collective-permute-done.11
  63.5 3.4 %collective-permute-start.13 = (bf16[384,512]{1,0:T(8,128)(2,1)S(1)}, bf16[384,512]{1,0:T(8,128)(2,1)S(1)}, u32[]{:S(2)}, u32[]{:S(2)}) collective-permute-start(bf16[384,512]{1,0:T(8,128)(2,1)S(1)} %fusion.9.refs_1_.refs_10_), channel_id=1, source_target_pairs={{0,16},{2,18},{4,20},{6,22},{8,24},{10,26},{12,28},{14,30},{16,0},... | collective-permute-start | bytes 1179656 | tf_op jit(solution)/shard_map/ppermute | solution.py:374
  72.3 3.5 %shard_map.316 = (f32[3,8,512]{2,1,0:T(8,128)S(1)}, f32[3,8,512]{2,1,0:T(8,128)S(1)}, f32[192,512]{1,0:T(8,128)S(1)}) custom-call(bf16[192,512]{1,0:T(8,128)(2,1)S(1)} %fusion.15.refs_0_, bf16[384,512]{1,0:T(8,128)(2,1)S(1)} %fusion.9.refs_1_.refs_10_, bf16[384,512]{1,0:T(8,128)(2,1)S(1)} %collective-permute-done.17.refs_2_.refs_11_), custom_call_target="tpu_custom_call" | custom-call | flops 350000000 | bytes 350000 | tf_op jit(solution)/shard_map/pallas_call | solution.py:471
  75.9 4.0 %shard_map.315 = (bf16[192,512]{1,0:T(8,128)(2,1)S(1)}, f32[3,8,512]{2,1,0:T(8,128)S(1)}) custom-call(s32[1]{0:T(128)} %bitcast.25.refs_0_, bf16[192,512]{1,0:T(8,128)(2,1)S(1)} %fusion.14.refs_1_, bf16[384,512]{1,0:T(8,128)(2,1)S(1)} %fusion.10.refs_2_.refs_5_, bf16[384,512]{1,0:T(8,128)(2,1)S(1)} %collective-permute-done.16.refs_3_.refs_6_), custom_call_target="tpu_custom_call" | custom-call | flops 350000000 | bytes 350000 | tf_op jit(solution)/shard_map/pallas_call | solution.py:471
  80.5 4.5 %collective-permute-done.13.refs_1_.refs_6_ = bf16[384,512]{1,0:T(8,128)(2,1)S(1)} collective-permute-done((bf16[384,512]{1,0:T(8,128)(2,1)S(1)}, bf16[384,512]{1,0:T(8,128)(2,1)S(1)}, u32[]{:S(2)}, u32[]{:S(2)}) %collective-permute-start.13) | collective-permute-done | bytes 393248 | tf_op jit(solution)/shard_map/ppermute | solution.py:374
  89.4 3.5 %shard_map.317 = (f32[3,8,512]{2,1,0:T(8,128)S(1)}, f32[3,8,512]{2,1,0:T(8,128)S(1)}, f32[192,512]{1,0:T(8,128)S(1)}) custom-call(bf16[192,512]{1,0:T(8,128)(2,1)S(1)} %fusion.15.refs_0_, bf16[384,512]{1,0:T(8,128)(2,1)S(1)} %collective-permute-done.12.refs_1_.refs_8_, bf16[384,512]{1,0:T(8,128)(2,1)S(1)} %collective-permute-done.20.refs_2_.refs_9_, ...), custom_call_target="tpu_custom_call" | custom-call | flops 350000000 | bytes 350000 | tf_op jit(solution)/shard_map/pallas_call | solution.py:471
  93.0 3.5 %shard_map.318 = (f32[3,8,512]{2,1,0:T(8,128)S(1)}, f32[3,8,512]{2,1,0:T(8,128)S(1)}, f32[192,512]{1,0:T(8,128)S(1)}) custom-call(bf16[192,512]{1,0:T(8,128)(2,1)S(1)} %fusion.15.refs_0_, bf16[384,512]{1,0:T(8,128)(2,1)S(1)} %collective-permute-done.13.refs_1_.refs_6_, bf16[384,512]{1,0:T(8,128)(2,1)S(1)} %collective-permute-done.19.refs_2_.refs_7_, ...), custom_call_target="tpu_custom_call" | custom-call | flops 350000000 | bytes 350000 | tf_op jit(solution)/shard_map/pallas_call | solution.py:471
  99.7 3.5 %shard_map.319 = (bf16[192,512]{1,0:T(8,128)(2,1)S(1)}, f32[3,8,512]{2,1,0:T(8,128)S(1)}) custom-call(bf16[192,512]{1,0:T(8,128)(2,1)S(1)} %fusion.15.refs_0_, bf16[384,512]{1,0:T(8,128)(2,1)S(1)} %collective-permute-done.18.refs_1_.refs_4_, bf16[384,512]{1,0:T(8,128)(2,1)S(1)} %collective-permute-done.21.refs_2_.refs_5_, ...), custom_call_target="tpu_custom_call" | custom-call | flops 350000000 | bytes 350000 | tf_op jit(solution)/shard_map/pallas_call | solution.py:471
  105.0 4.1 %collective-permute-done.22.one_far = bf16[8,144,384]{2,1,0:T(8,128)(2,1)S(1)} collective-permute-done((bf16[8,144,384]{2,1,0:T(8,128)(2,1)S(1)}, bf16[8,144,384]{2,1,0:T(8,128)(2,1)S(1)}, u32[]{:S(2)}, u32[]{:S(2)}) %collective-permute-start.22) | collective-permute-done | bytes 884768 | tf_op jit(solution)/shard_map/ppermute | solution.py:386
  129.1 2.4 collective-permute-start.30
  133.1 9.7 %multiply_convert_fusion = (bf16[512,1536]{1,0:T(8,128)(2,1)S(1)}, f32[512,1536]{1,0:T(8,128)}, f32[512,1536]{1,0:T(8,128)}) fusion(f32[1536]{0:T(1024)S(1)} %slice_reduce_fusion, bf16[768,1536]{1,0:T(8,128)(2,1)S(1)} %bitcast.187, bf16[256,768]{1,0:T(8,128)(2,1)S(1)} %collective-permute-done.27, bf16[256,768]{1,0:T(8,128)(2,1)S(1)} %fusion.42), kind=kOutput, calls=%fused_computation.6 | convolution fusion | flops 1261436928 | bytes 11016192 | tf_op jit(solution)/shard_map/dot_general | solution.py:32
  150.8 3.4 %fusion.92 = (f32[256]{0:T(256)S(1)}, f32[256,768]{1,0:T(8,128)S(1)}, f32[256,768]{1,0:T(8,128)}) fusion(f32[768]{0:T(1024)} %copy-done.97, f32[768]{0:T(1024)S(1)} %get-tuple-element.266, f32[256]{0:T(256)} %copy-done.98, f32[256,768]{1,0:T(8,128)} %copy-done.44, f32[256]{0:T(256)} %copy-done.91, f32[768]{0:T(1024)} %get-tuple-element.264, ...), kind=kOutput, calls=%fused_computation.281 | convolution fusion | flops 605748992 | bytes 5912576 | tf_op jit(solution)/shard_map/dot_general | solution.py:32
  159.1 2.9 convert_reduce_fusion
  177.6 4.5 %collective-permute-done.37 = bf16[384,256]{1,0:T(8,128)(2,1)S(1)} collective-permute-done((bf16[384,256]{1,0:T(8,128)(2,1)S(1)}, bf16[384,256]{1,0:T(8,128)(2,1)S(1)}, u32[]{:S(2)}, u32[]{:S(2)}) %collective-permute-start.37) | collective-permute-done | bytes 196640 | tf_op jit(solution)/shard_map/ppermute | solution.py:374
  195.3 20.3 %shard_map.322 = (f32[192,512]{1,0:T(8,128)S(1)}, bf16[384,512]{1,0:T(8,128)(2,1)S(1)}, bf16[384,512]{1,0:T(8,128)(2,1)S(1)}, bf16[384,512]{1,0:T(8,128)(2,1)S(1...) custom-call(bf16[192,512]{1,0:T(8,128)(2,1)S(1)} %fusion.15.refs_0_,, ...), custom_call_target="tpu_custom_call" | custom-call | flops 1000000000 | bytes 1000000 | tf_op jit(solution)/shard_map/pallas_call | solution.py:544
  218.3 5.7 %shard_map.323 = (f32[192,512]{1,0:T(8,128)S(1)}, bf16[384,512]{1,0:T(8,128)(2,1)S(1)}, bf16[384,512]{1,0:T(8,128)(2,1)S(1)}) custom-call(s32[1]{0:T(128)} %bitcast.25.refs_0_, bf16[192,512]{1,0:T(8,128)(2,1)S(1)} %copy-done.41, bf16[192,512]{1,0:T(8,128)(2,1)S(1)} %pad_maximum_fusion.28.refs_2_, f32[3,8,512]{2,1,0:T(8,128)S(1)} %copy-done.43, ...), custom_call_target="tpu_custom_call" | custom-call | flops 1000000000 | bytes 1000000 | tf_op jit(solution)/shard_map/pallas_call | solution.py:544
  232.7 5.3 %collective-permute-done.44 = bf16[384,512]{1,0:T(8,128)(2,1)S(1)} collective-permute-done((bf16[384,512]{1,0:T(8,128)(2,1)S(1)}, bf16[384,512]{1,0:T(8,128)(2,1)S(1)}, u32[]{:S(2)}, u32[]{:S(2)}) %collective-permute-start.44) | collective-permute-done | bytes 393248 | tf_op jit(solution)/shard_map/ppermute | solution.py:374
  239.9 6.1 %collective-permute-done.48 = bf16[4,192,384]{2,1,0:T(8,128)(2,1)S(1)} collective-permute-done((bf16[4,192,384]{2,1,0:T(8,128)(2,1)S(1)}, bf16[4,192,384]{2,1,0:T(8,128)(2,1)S(1)}, u32[]{:S(2)}, u32[]{:S(2)}) %collective-permute-start.48) | collective-permute-done | bytes 589856 | tf_op jit(solution)/shard_map/ppermute | solution.py:386
  246.3 4.8 %collective-permute-done.47 = bf16[4,240,384]{2,1,0:T(8,128)(2,1)S(1)} collective-permute-done((bf16[4,240,384]{2,1,0:T(8,128)(2,1)S(1)}, bf16[4,240,384]{2,1,0:T(8,128)(2,1)S(1)}, u32[]{:S(2)}, u32[]{:S(2)}) %collective-permute-start.47) | collective-permute-done | bytes 737312 | tf_op jit(solution)/shard_map/ppermute | solution.py:374
  255.0 2.4 collective-permute-done.50
  258.1 6.3 %collective-permute-done.49 = bf16[432,384]{1,0:T(8,128)(2,1)S(1)} collective-permute-done((bf16[432,384]{1,0:T(8,128)(2,1)S(1)}, bf16[432,384]{1,0:T(8,128)(2,1)S(1)}, u32[]{:S(2)}, u32[]{:S(2)}) %collective-permute-start.49) | collective-permute-done | bytes 331808 | tf_op jit(solution)/shard_map/ppermute | solution.py:374
  271.9 2.1 collective-permute-start.55
  274.0 5.5 %collective-permute-done.59 = bf16[2,56,576]{2,1,0:T(8,128)(2,1)S(1)} collective-permute-done((bf16[2,56,576]{2,1,0:T(8,128)(2,1)S(1)}, bf16[2,56,576]{2,1,0:T(8,128)(2,1)S(1)}, u32[]{:S(2)}, u32[]{:S(2)}) %collective-permute-start.59) | collective-permute-done | bytes 129056 | tf_op jit(solution)/shard_map/ppermute | solution.py:374
  279.6 2.4 collective-permute-done.53
  283.7 14.0 %collective-permute-done.58 = bf16[2,56,576]{2,1,0:T(8,128)(2,1)S(1)} collective-permute-done((bf16[2,56,576]{2,1,0:T(8,128)(2,1)S(1)}, bf16[2,56,576]{2,1,0:T(8,128)(2,1)S(1)}, u32[]{:S(2)}, u32[]{:S(2)}) %collective-permute-start.58) | collective-permute-done | bytes 129056 | tf_op jit(solution)/shard_map/ppermute | solution.py:374
  (486 shorter events, 134.4 us)
Async XLA Ops:
  7.1 12.3 %collective-permute-start.3 = (bf16[256,768]{1,0:T(8,128)(2,1)S(1)}, bf16[256,768]{1,0:T(8,128)(2,1)S(1)}, u32[]{:S(2)}, u32[]{:S(2)}) collective-permute-start(bf16[256,768]{1,0:T(8,128)(2,1)S(1)} %bitcast.199), channel_id=1, source_target_pairs={{0,1},{1,0},{2,3},{3,2},{4,5},{5,4},{6,7},{7,6},{8,9},{9,8},{10,11... | collective-permute-start | bytes 1179656 | tf_op jit(solution)/shard_map/ppermute | solution.py:386
  19.7 24.8 %collective-permute-start.6 = (bf16[256,768]{1,0:T(8,128)(2,1)S(1)}, bf16[256,768]{1,0:T(8,128)(2,1)S(1)}, u32[]{:S(2)}, u32[]{:S(2)}) collective-permute-start(bf16[256,768]{1,0:T(8,128)(2,1)S(1)} %get-tuple-element.142), channel_id=1, source_target_pairs={{0,4},{2,6},{4,0},{6,2},{8,12},{10,14},{12,8},{14,10},{16,20},{18,... | collective-permute-start | bytes 1179656 | tf_op jit(solution)/shard_map/ppermute | solution.py:374
  21.3 23.9 %collective-permute-start.8 = (bf16[432,384]{1,0:T(8,128)(2,1)S(1)}, bf16[432,384]{1,0:T(8,128)(2,1)S(1)}, u32[]{:S(2)}, u32[]{:S(2)}) collective-permute-start(bf16[432,384]{1,0:T(8,128)(2,1)S(1)} %fusion.64), channel_id=1, source_target_pairs={{0,16},{2,18},{4,20},{6,22},{8,24},{10,26},{12,28},{14,30},{16,0},... | collective-permute-start | bytes 995336 | tf_op jit(solution)/shard_map/ppermute | solution.py:374
  23.9 11.2 %collective-permute-start.4 = (bf16[2,56,576]{2,1,0:T(8,128)(2,1)S(1)}, bf16[2,56,576]{2,1,0:T(8,128)(2,1)S(1)}, u32[]{:S(2)}, u32[]{:S(2)}) collective-permute-start(bf16[2,56,576]{2,1,0:T(8,128)(2,1)S(1)} %get-tuple-element.342), channel_id=1, source_target_pairs={{0,8},{2,10},{4,12},{6,14},{8,0},{10,2},{12,4},{14,6},{16,24},{18,... | collective-permute-start | bytes 387080 | tf_op jit(solution)/shard_map/ppermute | solution.py:374
  25.6 19.0 %collective-permute-start.5 = (bf16[2,56,576]{2,1,0:T(8,128)(2,1)S(1)}, bf16[2,56,576]{2,1,0:T(8,128)(2,1)S(1)}, u32[]{:S(2)}, u32[]{:S(2)}) collective-permute-start(bf16[2,56,576]{2,1,0:T(8,128)(2,1)S(1)} %get-tuple-element.342), channel_id=1, source_target_pairs={{0,16},{2,18},{4,20},{6,22},{8,24},{10,26},{12,28},{14,30},{16,0},... | collective-permute-start | bytes 387080 | tf_op jit(solution)/shard_map/ppermute | solution.py:374
  50.9 10.3 %collective-permute-start.10 = (bf16[432,384]{1,0:T(8,128)(2,1)S(1)}, bf16[432,384]{1,0:T(8,128)(2,1)S(1)}, u32[]{:S(2)}, u32[]{:S(2)}) collective-permute-start(bf16[432,384]{1,0:T(8,128)(2,1)S(1)} %collective-permute-done.8), channel_id=1, source_target_pairs={{0,8},{2,10},{4,12},{6,14},{8,0},{10,2},{12,4},{14,6},{16,24},{18,... | collective-permute-start | bytes 995336 | tf_op jit(solution)/shard_map/ppermute | solution.py:374
  52.2 11.2 %collective-permute-start.11 = (bf16[256,768]{1,0:T(8,128)(2,1)S(1)}, bf16[256,768]{1,0:T(8,128)(2,1)S(1)}, u32[]{:S(2)}, u32[]{:S(2)}) collective-permute-start(bf16[256,768]{1,0:T(8,128)(2,1)S(1)} %get-tuple-element.152), channel_id=1, source_target_pairs={{0,4},{2,6},{4,0},{6,2},{8,12},{10,14},{12,8},{14,10},{16,20},{18,... | collective-permute-start | bytes 1179656 | tf_op jit(solution)/shard_map/ppermute | solution.py:374
  63.5 21.5 %collective-permute-start.13 = (bf16[384,512]{1,0:T(8,128)(2,1)S(1)}, bf16[384,512]{1,0:T(8,128)(2,1)S(1)}, u32[]{:S(2)}, u32[]{:S(2)}) collective-permute-start(bf16[384,512]{1,0:T(8,128)(2,1)S(1)} %fusion.9.refs_1_.refs_10_), channel_id=1, source_target_pairs={{0,16},{2,18},{4,20},{6,22},{8,24},{10,26},{12,28},{14,30},{16,0},... | collective-permute-start | bytes 1179656 | tf_op jit(solution)/shard_map/ppermute | solution.py:374
  66.9 19.5 %collective-permute-start.12 = (bf16[384,512]{1,0:T(8,128)(2,1)S(1)}, bf16[384,512]{1,0:T(8,128)(2,1)S(1)}, u32[]{:S(2)}, u32[]{:S(2)}) collective-permute-start(bf16[384,512]{1,0:T(8,128)(2,1)S(1)} %fusion.9.refs_1_.refs_10_), channel_id=1, source_target_pairs={{0,8},{2,10},{4,12},{6,14},{8,0},{10,2},{12,4},{14,6},{16,24},{18,... | collective-permute-start | bytes 1179656 | tf_op jit(solution)/shard_map/ppermute | solution.py:374
  68.5 18.0 %collective-permute-start.14 = (bf16[4,144,384]{2,1,0:T(8,128)(2,1)S(1)}, bf16[4,144,384]{2,1,0:T(8,128)(2,1)S(1)}, u32[]{:S(2)}, u32[]{:S(2)}) collective-permute-start(bf16[4,144,384]{2,1,0:T(8,128)(2,1)S(1)} %slice.420), channel_id=1, source_target_pairs={{0,4},{2,6},{4,0},{6,2},{8,12},{10,14},{12,8},{14,10},{16,20},{18,... | collective-permute-start | bytes 1327112 | tf_op jit(solution)/shard_map/ppermute | solution.py:374
  70.4 10.1 %collective-permute-start.15 = (bf16[4,96,384]{2,1,0:T(8,128)(2,1)S(1)}, bf16[4,96,384]{2,1,0:T(8,128)(2,1)S(1)}, u32[]{:S(2)}, u32[]{:S(2)}) collective-permute-start(bf16[4,96,384]{2,1,0:T(8,128)(2,1)S(1)} %get-tuple-element.291), channel_id=1, source_target_pairs={{0,1},{1,0},{2,3},{3,2},{4,5},{5,4},{6,7},{7,6},{8,9},{9,8},{10,11... | collective-permute-start | bytes 884744 | tf_op jit(solution)/shard_map/ppermute | solution.py:386
  86.5 11.5 %collective-permute-start.18 = (bf16[384,512]{1,0:T(8,128)(2,1)S(1)}, bf16[384,512]{1,0:T(8,128)(2,1)S(1)}, u32[]{:S(2)}, u32[]{:S(2)}) collective-permute-start(bf16[384,512]{1,0:T(8,128)(2,1)S(1)} %collective-permute-done.13.refs_1_.refs_6_), channel_id=1, source_target_pairs={{0,8},{2,10},{4,12},{6,14},{8,0},{10,2},{12,4},{14,6},{16,24},{18,... | collective-permute-start | bytes 1179656 | tf_op jit(solution)/shard_map/ppermute | solution.py:374
  87.2 22.0 %collective-permute-start.22 = (bf16[8,144,384]{2,1,0:T(8,128)(2,1)S(1)}, bf16[8,144,384]{2,1,0:T(8,128)(2,1)S(1)}, u32[]{:S(2)}, u32[]{:S(2)}) collective-permute-start(bf16[8,144,384]{2,1,0:T(8,128)(2,1)S(1)} %pad_maximum_fusion.3.one_own), channel_id=1, source_target_pairs={{0,1},{1,0},{2,3},{3,2},{4,5},{5,4},{6,7},{7,6},{8,9},{9,8},{10,11... | collective-permute-start | bytes 2654216 | tf_op jit(solution)/shard_map/ppermute | solution.py:386
  88.8 15.4 %collective-permute-start.23 = (bf16[2,4,96,384]{3,2,1,0:T(8,128)(2,1)S(1)}, bf16[2,4,96,384]{3,2,1,0:T(8,128)(2,1)S(1)}, u32[]{:S(2)}, u32[]{:S(2)}) collective-permute-start(bf16[2,4,96,384]{3,2,1,0:T(8,128)(2,1)S(1)} %pad_maximum_fusion.6.two_own), channel_id=1, source_target_pairs={{0,4},{2,6},{4,0},{6,2},{8,12},{10,14},{12,8},{14,10},{16,20},{18,... | collective-permute-start | bytes 1769480 | tf_op jit(solution)/shard_map/ppermute | solution.py:374
  129.1 15.8 %collective-permute-start.30 = (bf16[8,96,384]{2,1,0:T(8,128)(2,1)S(1)}, bf16[8,96,384]{2,1,0:T(8,128)(2,1)S(1)}, u32[]{:S(2)}, u32[]{:S(2)}) collective-permute-start(bf16[8,96,384]{2,1,0:T(8,128)(2,1)S(1)} %constant_dynamic-update-slice_fusion.4.one_own), channel_id=1, source_target_pairs={{0,1},{1,0},{2,3},{3,2},{4,5},{5,4},{6,7},{7,6},{8,9},{9,8},{10,11... | collective-permute-start | bytes 1769480 | tf_op jit(solution)/shard_map/ppermute | solution.py:386
  131.6 14.9 %collective-permute-start.31 = (bf16[2,4,96,384]{3,2,1,0:T(8,128)(2,1)S(1)}, bf16[2,4,96,384]{3,2,1,0:T(8,128)(2,1)S(1)}, u32[]{:S(2)}, u32[]{:S(2)}) collective-permute-start(bf16[2,4,96,384]{3,2,1,0:T(8,128)(2,1)S(1)} %pad_maximum_fusion.7.two_own), channel_id=1, source_target_pairs={{0,4},{2,6},{4,0},{6,2},{8,12},{10,14},{12,8},{14,10},{16,20},{18,... | collective-permute-start | bytes 1769480 | tf_op jit(solution)/shard_map/ppermute | solution.py:374
  169.2 14.2 %collective-permute-start.35 = (bf16[4,2,48,768]{3,2,0,1:T(8,128)(2,1)S(1)}, bf16[4,2,48,768]{3,2,0,1:T(8,128)(2,1)S(1)}, u32[]{:S(2)}, u32[]{:S(2)}) collective-permute-start(bf16[4,2,48,768]{3,2,0,1:T(8,128)(2,1)S(1)} %select_bitcast_fusion.2), channel_id=1, source_target_pairs={{0,2},{2,0},{4,6},{6,4},{8,10},{10,8},{12,14},{14,12},{16,18},{18,... | collective-permute-start | bytes 1769480 | tf_op jit(solution)/shard_map/ppermute | solution.py:374
  185.9 38.1 %collective-permute-start.42 = (bf16[4,2,240,384]{3,2,0,1:T(8,128)(2,1)}, bf16[4,2,240,384]{3,2,0,1:T(8,128)(2,1)}, u32[]{:S(2)}, u32[]{:S(2)}) collective-permute-start(bf16[4,2,240,384]{3,2,0,1:T(8,128)(2,1)} %pad_maximum_fusion), channel_id=1, source_target_pairs={{0,1},{1,0},{2,3},{3,2},{4,5},{5,4},{6,7},{7,6},{8,9},{9,8},{10,11... | collective-permute-start | bytes 4423688 | tf_op jit(solution)/shard_map/ppermute | solution.py:386
  186.5 37.5 %collective-permute-start.43 = (bf16[4,192,768]{2,1,0:T(8,128)(2,1)}, bf16[4,192,768]{2,1,0:T(8,128)(2,1)}, u32[]{:S(2)}, u32[]{:S(2)}) collective-permute-start(bf16[4,192,768]{2,1,0:T(8,128)(2,1)} %select_bitcast_fusion), channel_id=1, source_target_pairs={{0,4},{2,6},{4,0},{6,2},{8,12},{10,14},{12,8},{14,10},{16,20},{18,... | collective-permute-start | bytes 3538952 | tf_op jit(solution)/shard_map/ppermute | solution.py:374
  226.0 12.0 %collective-permute-start.44 = (bf16[384,512]{1,0:T(8,128)(2,1)S(1)}, bf16[384,512]{1,0:T(8,128)(2,1)S(1)}, u32[]{:S(2)}, u32[]{:S(2)}) collective-permute-start(bf16[384,512]{1,0:T(8,128)(2,1)S(1)} %add_convert_fusion.9), channel_id=1, source_target_pairs={{0,8},{2,10},{4,12},{6,14},{8,0},{10,2},{12,4},{14,6},{16,24},{18,... | collective-permute-start | bytes 1179656 | tf_op jit(solution)/shard_map/ppermute | solution.py:374
  226.2 31.9 %collective-permute-start.46 = (bf16[384,512]{1,0:T(8,128)(2,1)S(1)}, bf16[384,512]{1,0:T(8,128)(2,1)S(1)}, u32[]{:S(2)}, u32[]{:S(2)}) collective-permute-start(bf16[384,512]{1,0:T(8,128)(2,1)S(1)} %add_convert_fusion.7), channel_id=1, source_target_pairs={{0,8},{2,10},{4,12},{6,14},{8,0},{10,2},{12,4},{14,6},{16,24},{18,... | collective-permute-start | bytes 1179656 | tf_op jit(solution)/shard_map/ppermute | solution.py:374
  230.3 15.7 %collective-permute-start.48 = (bf16[4,192,384]{2,1,0:T(8,128)(2,1)S(1)}, bf16[4,192,384]{2,1,0:T(8,128)(2,1)S(1)}, u32[]{:S(2)}, u32[]{:S(2)}) collective-permute-start(bf16[4,192,384]{2,1,0:T(8,128)(2,1)S(1)} %broadcast_select_fusion), channel_id=1, source_target_pairs={{0,1},{1,0},{2,3},{3,2},{4,5},{5,4},{6,7},{7,6},{8,9},{9,8},{10,11... | collective-permute-start | bytes 1769480 | tf_op jit(solution)/shard_map/ppermute | solution.py:386
  231.8 19.3 %collective-permute-start.47 = (bf16[4,240,384]{2,1,0:T(8,128)(2,1)S(1)}, bf16[4,240,384]{2,1,0:T(8,128)(2,1)S(1)}, u32[]{:S(2)}, u32[]{:S(2)}) collective-permute-start(bf16[4,240,384]{2,1,0:T(8,128)(2,1)S(1)} %select_bitcast_fusion.1), channel_id=1, source_target_pairs={{0,4},{2,6},{4,0},{6,2},{8,12},{10,14},{12,8},{14,10},{16,20},{18,... | collective-permute-start | bytes 2211848 | tf_op jit(solution)/shard_map/ppermute | solution.py:374
  238.2 19.9 %collective-permute-start.45 = (bf16[384,512]{1,0:T(8,128)(2,1)S(1)}, bf16[384,512]{1,0:T(8,128)(2,1)S(1)}, u32[]{:S(2)}, u32[]{:S(2)}) collective-permute-start(bf16[384,512]{1,0:T(8,128)(2,1)S(1)} %add_convert_fusion.8), channel_id=1, source_target_pairs={{0,16},{2,18},{4,20},{6,22},{8,24},{10,26},{12,28},{14,30},{16,0},... | collective-permute-start | bytes 1179656 | tf_op jit(solution)/shard_map/ppermute | solution.py:374
  239.3 25.2 %collective-permute-start.52 = (bf16[256,768]{1,0:T(8,128)(2,1)S(1)}, bf16[256,768]{1,0:T(8,128)(2,1)S(1)}, u32[]{:S(2)}, u32[]{:S(2)}) collective-permute-start(bf16[256,768]{1,0:T(8,128)(2,1)S(1)} %slice.661), channel_id=1, source_target_pairs={{0,4},{2,6},{4,0},{6,2},{8,12},{10,14},{12,8},{14,10},{16,20},{18,... | collective-permute-start | bytes 1179656 | tf_op jit(solution)/shard_map/ppermute | solution.py:374
  254.3 10.1 %collective-permute-start.49 = (bf16[432,384]{1,0:T(8,128)(2,1)S(1)}, bf16[432,384]{1,0:T(8,128)(2,1)S(1)}, u32[]{:S(2)}, u32[]{:S(2)}) collective-permute-start(bf16[432,384]{1,0:T(8,128)(2,1)S(1)} %get-tuple-element.287), channel_id=1, source_target_pairs={{0,8},{2,10},{4,12},{6,14},{8,0},{10,2},{12,4},{14,6},{16,24},{18,... | collective-permute-start | bytes 995336 | tf_op jit(solution)/shard_map/ppermute | solution.py:374
  270.6 11.4 %collective-permute-start.53 = (bf16[256,768]{1,0:T(8,128)(2,1)S(1)}, bf16[256,768]{1,0:T(8,128)(2,1)S(1)}, u32[]{:S(2)}, u32[]{:S(2)}) collective-permute-start(bf16[256,768]{1,0:T(8,128)(2,1)S(1)} %slice.660), channel_id=1, source_target_pairs={{0,4},{2,6},{4,0},{6,2},{8,12},{10,14},{12,8},{14,10},{16,20},{18,... | collective-permute-start | bytes 1179656 | tf_op jit(solution)/shard_map/ppermute | solution.py:374
  271.8 26.1 %collective-permute-start.56 = (bf16[432,384]{1,0:T(8,128)(2,1)S(1)}, bf16[432,384]{1,0:T(8,128)(2,1)S(1)}, u32[]{:S(2)}, u32[]{:S(2)}) collective-permute-start(bf16[432,384]{1,0:T(8,128)(2,1)S(1)} %add_convert_fusion.13), channel_id=1, source_target_pairs={{0,16},{2,18},{4,20},{6,22},{8,24},{10,26},{12,28},{14,30},{16,0},... | collective-permute-start | bytes 995336 | tf_op jit(solution)/shard_map/ppermute | solution.py:374
  271.9 26.0 %collective-permute-start.55 = (bf16[432,384]{1,0:T(8,128)(2,1)S(1)}, bf16[432,384]{1,0:T(8,128)(2,1)S(1)}, u32[]{:S(2)}, u32[]{:S(2)}) collective-permute-start(bf16[432,384]{1,0:T(8,128)(2,1)S(1)} %copy-done.86), channel_id=1, source_target_pairs={{0,8},{2,10},{4,12},{6,14},{8,0},{10,2},{12,4},{14,6},{16,24},{18,... | collective-permute-start | bytes 995336 | tf_op jit(solution)/shard_map/ppermute | solution.py:374
  274.0 23.8 %collective-permute-start.58 = (bf16[2,56,576]{2,1,0:T(8,128)(2,1)S(1)}, bf16[2,56,576]{2,1,0:T(8,128)(2,1)S(1)}, u32[]{:S(2)}, u32[]{:S(2)}) collective-permute-start(bf16[2,56,576]{2,1,0:T(8,128)(2,1)S(1)} %get-tuple-element.311), channel_id=1, source_target_pairs={{0,8},{2,10},{4,12},{6,14},{8,0},{10,2},{12,4},{14,6},{16,24},{18,... | collective-permute-start | bytes 387080 | tf_op jit(solution)/shard_map/ppermute | solution.py:374
  279.5 18.2 %collective-permute-start.60 = (bf16[2,56,576]{2,1,0:T(8,128)(2,1)S(1)}, bf16[2,56,576]{2,1,0:T(8,128)(2,1)S(1)}, u32[]{:S(2)}, u32[]{:S(2)}) collective-permute-start(bf16[2,56,576]{2,1,0:T(8,128)(2,1)S(1)} %fusion.65), channel_id=1, source_target_pairs={{0,16},{2,18},{4,20},{6,22},{8,24},{10,26},{12,28},{14,30},{16,0},... | collective-permute-start | bytes 387080 | tf_op jit(solution)/shard_map/ppermute | solution.py:374
  282.2 18.7 %collective-permute-start.54 = (bf16[256,768]{1,0:T(8,128)(2,1)S(1)}, bf16[256,768]{1,0:T(8,128)(2,1)S(1)}, u32[]{:S(2)}, u32[]{:S(2)}) collective-permute-start(bf16[256,768]{1,0:T(8,128)(2,1)S(1)} %select_convert_fusion), channel_id=1, source_target_pairs={{0,1},{1,0},{2,3},{3,2},{4,5},{5,4},{6,7},{7,6},{8,9},{9,8},{10,11... | collective-permute-start | bytes 1179656 | tf_op jit(solution)/shard_map/ppermute | solution.py:386
  (143 other events, 841.0 us)

commit v2 on v1

--- a/solution.py
+++ b/solution.py
@@ -745,7 +745,7 @@
     z_one, z_two, long_far, short_own = hold(
         ctx_move(own_block, 4), ctx_move(own_block, 8), y_swap(long_own), short_own
     )
-    z_three, ffn_two = hold(ctx_move(z_two, 4), ffn_two)
+    z_three = ctx_move(z_two, 4)
     ffn_three = ctx_move(ffn_two, 4)
     z_stack = jnp.stack([own_block, z_one, z_two, z_three])
     qkv_weight, wide, heads, hidden = place_call(
@@ -927,7 +927,22 @@
         long_query, long_grad, long_log, long_mixed, sum(pairs[::-1], ())
     )
     near, far = grads[::2], grads[1::2]
-    short_query_b, grad_query = hold(short_query, grad_query)
+    *far, grad_query, in_x, down_y = hold(
+        *(core_swap(part) for part in far), grad_query, in_x, down_y
+    )
+    three, two, one = (add_b(near[i], far[i]) for i in range(3))
+    near_own, far_own = near[3], far[3]
+    in_sum = add_b(in_keep_grad, in_x)
+    down_sum = add_b(down_keep, down_y)
+    three_hop = ctx_move(three, 4)
+    in_send = jnp.where(y_low, in_sum[:, 1], in_sum[:, 0])
+    down_send = jnp.where(x_low, down_sum[..., 384:], down_sum[..., :384])
+    in_send, down_send, two = hold(in_send, down_send, two)
+    short_query_b, three_hop = hold(short_query, three_hop)
+    in_y, down_x = y_swap(in_send), x_swap(down_send)
+    one, three_hop = hold(one, three_hop)
+    two_got = ctx_move(add_b(two, three_hop), 8)
+    one_got = ctx_move(one, 4)
     short_back = attend_back_call(
         short_query_b,
         short_grad,
@@ -936,19 +951,7 @@
         short_pairs,
         flag=short_flag,
     )
-    *far, grad_query, in_x, down_y, short_query_g, short_near, short_far = hold(
-        *(core_swap(part) for part in far), grad_query, in_x, down_y, *short_back
-    )
-    three, two, one = (add_b(near[i], far[i]) for i in range(3))
-    near_own, far_own = near[3], far[3]
-    in_sum = add_b(in_keep_grad, in_x)
-    down_sum = add_b(down_keep, down_y)
-    three_hop, one_got = ctx_move(three, 4), ctx_move(one, 4)
-    two_got = ctx_move(add_b(two, three_hop), 8)
-    in_send = jnp.where(y_low, in_sum[:, 1], in_sum[:, 0])
-    down_send = jnp.where(x_low, down_sum[..., 384:], down_sum[..., :384])
-    in_send, down_send, short_far = hold(in_send, down_send, short_far)
-    in_y, down_x = y_swap(in_send), x_swap(down_send)
+    short_query_g, short_near, short_far = short_back
     short_pair_grad = add_b(short_near, core_swap(short_far))
     stream, attn_branch, ffn_branch, in_y = hold(stream, attn_branch, ffn_branch, in_y)
     (

time: 316 us -> 313 us (level)
  waiting for transfers between devices: 118 us -> 110 us
  starting transfers between devices: 48.1 us -> 52.7 us
    ppermute x11, waiting for transfers between devices: 24.2 us -> 17.4 us  [x_swap(): return lax.ppermute(value, 'fsdp', [(0, 1), (1, 0)])]
    ppermute x52, starting transfers between devices: 33.3 us -> 38.7 us  [ctx_move(): return lax.ppermute(value, 'ctx', [(i, i ^ mask) for i in range(16)])]
    unnamed x227 -> x223, local copies, waits for them, and re-layouts: 14.3 us -> 12.5 us
  transfers between devices with their start and end apart: 63 -> 63, of which waited for: 32 -> 35; matrix products, arithmetic and copies ran while one was open for 16% -> 16% of each run, Pallas kernels for 15% -> 15%
where the time goes in v2:
time: 313 us; the launch traced here: 307 us
  waiting for transfers between devices  110 us (35%)
  starting transfers between devices  52.7 us (17%)
  Pallas kernels  49.2 us (16%)
  matrix products  35 us (11%)
  other arithmetic  27.9 us (9%)
  local copies, waits for them, and re-layouts  27 us (9%)
  between operations  4.89 us (2%)
    ppermute x52, waiting for transfers between devices, ctx_move(): return lax.ppermute(value, 'ctx', [(i, i ^ mask) for i in range(16)])  92.9 us
    ppermute x52, starting transfers between devices, ctx_move(): return lax.ppermute(value, 'ctx', [(i, i ^ mask) for i in range(16)])  38.7 us
    pallas_call x2, Pallas kernels, attend_back_call(): pl.pallas_call(functools.partial(attend_back_kernel, len(pairs), grad_que...  26 us
    pallas_call x5, Pallas kernels, attend_call(): pl.pallas_call(functools.partial(attend_kernel, len(pairs), state is None...  18.1 us
    ppermute x11, waiting for transfers between devices, x_swap(): return lax.ppermute(value, 'fsdp', [(0, 1), (1, 0)])  17.4 us
    dot_general x4, matrix products, plain_product(): return jnp.dot(left_side, right_side, preferred_element_type=jnp.float32)  15.1 us
    ppermute x11, starting transfers between devices, x_swap(): return lax.ppermute(value, 'fsdp', [(0, 1), (1, 0)])  14 us
    unnamed x223, local copies, waits for them, and re-layouts  12.5 us
  transfers between devices with their start and end apart: 63, of which 35 were waited for; matrix products, arithmetic and copies ran while one was open for 16% of the time, Pallas kernels for 15%

profile of v2, /device:TPU:0, one launch (start us, length us, event | category | flops | bytes accessed | tf_op | source)
XLA Modules:
  0.0 307.1 jit_solution(3110170992084162383)
XLA Ops:
  7.1 2.6 collective-permute-start.3
  13.6 5.8 %collective-permute-done.3 = bf16[256,768]{1,0:T(8,128)(2,1)S(1)} collective-permute-done((bf16[256,768]{1,0:T(8,128)(2,1)S(1)}, bf16[256,768]{1,0:T(8,128)(2,1)S(1)}, u32[]{:S(2)}, u32[]{:S(2)}) %collective-permute-start.3) | collective-permute-done | bytes 393248 | tf_op jit(solution)/shard_map/ppermute | solution.py:386
  23.0 2.6 collective-permute-start.5
  25.6 3.0 collective-permute-done.4
  28.6 3.2 %collective-permute-done.5 = bf16[2,56,576]{2,1,0:T(8,128)(2,1)S(1)} collective-permute-done((bf16[2,56,576]{2,1,0:T(8,128)(2,1)S(1)}, bf16[2,56,576]{2,1,0:T(8,128)(2,1)S(1)}, u32[]{:S(2)}, u32[]{:S(2)}) %collective-permute-start.5) | collective-permute-done | bytes 129056 | tf_op jit(solution)/shard_map/ppermute | solution.py:374
  32.1 2.7 collective-permute-start.9
  34.8 2.9 collective-permute-done.7
  37.9 10.3 %collective-permute-done.9 = bf16[432,384]{1,0:T(8,128)(2,1)S(1)} collective-permute-done((bf16[432,384]{1,0:T(8,128)(2,1)S(1)}, bf16[432,384]{1,0:T(8,128)(2,1)S(1)}, u32[]{:S(2)}, u32[]{:S(2)}) %collective-permute-start.9) | collective-permute-done | bytes 331808 | tf_op jit(solution)/shard_map/ppermute | solution.py:374
  52.6 3.8 %collective-permute-done.10 = bf16[432,384]{1,0:T(8,128)(2,1)S(1)} collective-permute-done((bf16[432,384]{1,0:T(8,128)(2,1)S(1)}, bf16[432,384]{1,0:T(8,128)(2,1)S(1)}, u32[]{:S(2)}, u32[]{:S(2)}) %collective-permute-start.10) | collective-permute-done | bytes 331808 | tf_op jit(solution)/shard_map/ppermute | solution.py:374
  58.8 2.7 collective-permute-start.13
  67.9 3.5 %shard_map.316 = (f32[3,8,512]{2,1,0:T(8,128)S(1)}, f32[3,8,512]{2,1,0:T(8,128)S(1)}, f32[192,512]{1,0:T(8,128)S(1)}) custom-call(bf16[192,512]{1,0:T(8,128)(2,1)S(1)} %fusion.15.refs_0_, bf16[384,512]{1,0:T(8,128)(2,1)S(1)} %fusion.9.refs_1_.refs_10_, bf16[384,512]{1,0:T(8,128)(2,1)S(1)} %collective-permute-done.17.refs_2_.refs_11_), custom_call_target="tpu_custom_call" | custom-call | flops 350000000 | bytes 350000 | tf_op jit(solution)/shard_map/pallas_call | solution.py:471
  71.5 4.0 %shard_map.315 = (bf16[192,512]{1,0:T(8,128)(2,1)S(1)}, f32[3,8,512]{2,1,0:T(8,128)S(1)}) custom-call(s32[1]{0:T(128)} %bitcast.25.refs_0_, bf16[192,512]{1,0:T(8,128)(2,1)S(1)} %fusion.14.refs_1_, bf16[384,512]{1,0:T(8,128)(2,1)S(1)} %fusion.10.refs_2_.refs_5_, bf16[384,512]{1,0:T(8,128)(2,1)S(1)} %collective-permute-done.16.refs_3_.refs_6_), custom_call_target="tpu_custom_call" | custom-call | flops 350000000 | bytes 350000 | tf_op jit(solution)/shard_map/pallas_call | solution.py:471
  76.1 3.7 %collective-permute-done.13.refs_1_.refs_6_ = bf16[384,512]{1,0:T(8,128)(2,1)S(1)} collective-permute-done((bf16[384,512]{1,0:T(8,128)(2,1)S(1)}, bf16[384,512]{1,0:T(8,128)(2,1)S(1)}, u32[]{:S(2)}, u32[]{:S(2)}) %collective-permute-start.13) | collective-permute-done | bytes 393248 | tf_op jit(solution)/shard_map/ppermute | solution.py:374
  85.1 3.5 %shard_map.317 = (f32[3,8,512]{2,1,0:T(8,128)S(1)}, f32[3,8,512]{2,1,0:T(8,128)S(1)}, f32[192,512]{1,0:T(8,128)S(1)}) custom-call(bf16[192,512]{1,0:T(8,128)(2,1)S(1)} %fusion.15.refs_0_, bf16[384,512]{1,0:T(8,128)(2,1)S(1)} %collective-permute-done.12.refs_1_.refs_8_, bf16[384,512]{1,0:T(8,128)(2,1)S(1)} %collective-permute-done.20.refs_2_.refs_9_, ...), custom_call_target="tpu_custom_call" | custom-call | flops 350000000 | bytes 350000 | tf_op jit(solution)/shard_map/pallas_call | solution.py:471
  88.6 3.5 %shard_map.318 = (f32[3,8,512]{2,1,0:T(8,128)S(1)}, f32[3,8,512]{2,1,0:T(8,128)S(1)}, f32[192,512]{1,0:T(8,128)S(1)}) custom-call(bf16[192,512]{1,0:T(8,128)(2,1)S(1)} %fusion.15.refs_0_, bf16[384,512]{1,0:T(8,128)(2,1)S(1)} %collective-permute-done.13.refs_1_.refs_6_, bf16[384,512]{1,0:T(8,128)(2,1)S(1)} %collective-permute-done.19.refs_2_.refs_7_, ...), custom_call_target="tpu_custom_call" | custom-call | flops 350000000 | bytes 350000 | tf_op jit(solution)/shard_map/pallas_call | solution.py:471
  94.0 3.5 %shard_map.319 = (bf16[192,512]{1,0:T(8,128)(2,1)S(1)}, f32[3,8,512]{2,1,0:T(8,128)S(1)}) custom-call(bf16[192,512]{1,0:T(8,128)(2,1)S(1)} %fusion.15.refs_0_, bf16[384,512]{1,0:T(8,128)(2,1)S(1)} %collective-permute-done.18.refs_1_.refs_4_, bf16[384,512]{1,0:T(8,128)(2,1)S(1)} %collective-permute-done.21.refs_2_.refs_5_, ...), custom_call_target="tpu_custom_call" | custom-call | flops 350000000 | bytes 350000 | tf_op jit(solution)/shard_map/pallas_call | solution.py:471
  99.7 4.2 %collective-permute-done.22.one_far = bf16[8,144,384]{2,1,0:T(8,128)(2,1)S(1)} collective-permute-done((bf16[8,144,384]{2,1,0:T(8,128)(2,1)S(1)}, bf16[8,144,384]{2,1,0:T(8,128)(2,1)S(1)}, u32[]{:S(2)}, u32[]{:S(2)}) %collective-permute-start.22) | collective-permute-done | bytes 884768 | tf_op jit(solution)/shard_map/ppermute | solution.py:386
  127.8 9.7 %multiply_convert_fusion = (bf16[512,1536]{1,0:T(8,128)(2,1)S(1)}, f32[512,1536]{1,0:T(8,128)}, f32[512,1536]{1,0:T(8,128)}) fusion(f32[1536]{0:T(1024)S(1)} %slice_reduce_fusion, bf16[768,1536]{1,0:T(8,128)(2,1)S(1)} %bitcast.187, bf16[256,768]{1,0:T(8,128)(2,1)S(1)} %collective-permute-done.27, bf16[256,768]{1,0:T(8,128)(2,1)S(1)} %fusion.42), kind=kOutput, calls=%fused_computation.6 | convolution fusion | flops 1261436928 | bytes 11016192 | tf_op jit(solution)/shard_map/dot_general | solution.py:32
  137.6 2.9 collective-permute-done.30.one_far
  146.4 3.4 %fusion.91 = (f32[256]{0:T(256)S(1)}, f32[256,768]{1,0:T(8,128)S(1)}, f32[256,768]{1,0:T(8,128)}) fusion(f32[768]{0:T(1024)} %copy-done.96, f32[768]{0:T(1024)S(1)} %get-tuple-element.260, f32[256]{0:T(256)} %copy-done.97, f32[256,768]{1,0:T(8,128)} %copy-done.49, f32[256]{0:T(256)} %copy-done.90, f32[768]{0:T(1024)} %get-tuple-element.258, ...), kind=kOutput, calls=%fused_computation.280 | convolution fusion | flops 605748992 | bytes 5912576 | tf_op jit(solution)/shard_map/dot_general | solution.py:32
  154.7 2.9 convert_reduce_fusion
  172.3 5.4 %collective-permute-done.37 = bf16[384,256]{1,0:T(8,128)(2,1)S(1)} collective-permute-done((bf16[384,256]{1,0:T(8,128)(2,1)S(1)}, bf16[384,256]{1,0:T(8,128)(2,1)S(1)}, u32[]{:S(2)}, u32[]{:S(2)}) %collective-permute-start.37) | collective-permute-done | bytes 196640 | tf_op jit(solution)/shard_map/ppermute | solution.py:374
  182.1 20.3 %shard_map.322 = (f32[192,512]{1,0:T(8,128)S(1)}, bf16[384,512]{1,0:T(8,128)(2,1)S(1)}, bf16[384,512]{1,0:T(8,128)(2,1)}, bf16[384,512]{1,0:T(8,128)(2,1)S(1)}, ...) custom-call(bf16[192,512]{1,0:T(8,128)(2,1)S(1)} %fusion.15.refs_0_,, ...), custom_call_target="tpu_custom_call" | custom-call | flops 1000000000 | bytes 1000000 | tf_op jit(solution)/shard_map/pallas_call | solution.py:544
  207.4 2.5 convolution_convert_fusion.1
  221.9 5.6 %collective-permute-done.44 = bf16[384,512]{1,0:T(8,128)(2,1)S(1)} collective-permute-done((bf16[384,512]{1,0:T(8,128)(2,1)S(1)}, bf16[384,512]{1,0:T(8,128)(2,1)S(1)}, u32[]{:S(2)}, u32[]{:S(2)}) %collective-permute-start.44) | collective-permute-done | bytes 393248 | tf_op jit(solution)/shard_map/ppermute | solution.py:374
  227.9 5.7 %shard_map.323 = (f32[192,512]{1,0:T(8,128)S(1)}, bf16[384,512]{1,0:T(8,128)(2,1)S(1)}, bf16[384,512]{1,0:T(8,128)(2,1)S(1)}) custom-call(s32[1]{0:T(128)} %bitcast.25.refs_0_, bf16[192,512]{1,0:T(8,128)(2,1)S(1)} %copy-done.46, bf16[192,512]{1,0:T(8,128)(2,1)S(1)} %pad_maximum_fusion.28.refs_2_, f32[3,8,512]{2,1,0:T(8,128)S(1)} %copy-done.48, ...), custom_call_target="tpu_custom_call" | custom-call | flops 1000000000 | bytes 1000000 | tf_op jit(solution)/shard_map/pallas_call | solution.py:544
  234.4 3.9 %collective-permute-done.47 = bf16[4,240,384]{2,1,0:T(8,128)(2,1)S(1)} collective-permute-done((bf16[4,240,384]{2,1,0:T(8,128)(2,1)S(1)}, bf16[4,240,384]{2,1,0:T(8,128)(2,1)S(1)}, u32[]{:S(2)}, u32[]{:S(2)}) %collective-permute-start.47) | collective-permute-done | bytes 737312 | tf_op jit(solution)/shard_map/ppermute | solution.py:374
  245.7 8.2 %collective-permute-done.45 = bf16[384,512]{1,0:T(8,128)(2,1)S(1)} collective-permute-done((bf16[384,512]{1,0:T(8,128)(2,1)S(1)}, bf16[384,512]{1,0:T(8,128)(2,1)S(1)}, u32[]{:S(2)}, u32[]{:S(2)}) %collective-permute-start.45) | collective-permute-done | bytes 393248 | tf_op jit(solution)/shard_map/ppermute | solution.py:374
  253.8 5.4 %collective-permute-done.49 = bf16[432,384]{1,0:T(8,128)(2,1)S(1)} collective-permute-done((bf16[432,384]{1,0:T(8,128)(2,1)S(1)}, bf16[432,384]{1,0:T(8,128)(2,1)S(1)}, u32[]{:S(2)}, u32[]{:S(2)}) %collective-permute-start.49) | collective-permute-done | bytes 331808 | tf_op jit(solution)/shard_map/ppermute | solution.py:374
  270.7 5.4 %collective-permute-done.59 = bf16[2,56,576]{2,1,0:T(8,128)(2,1)S(1)} collective-permute-done((bf16[2,56,576]{2,1,0:T(8,128)(2,1)S(1)}, bf16[2,56,576]{2,1,0:T(8,128)(2,1)S(1)}, u32[]{:S(2)}, u32[]{:S(2)}) %collective-permute-start.59) | collective-permute-done | bytes 129056 | tf_op jit(solution)/shard_map/ppermute | solution.py:374
  276.3 2.5 collective-permute-done.53
  280.4 14.0 %collective-permute-done.58 = bf16[2,56,576]{2,1,0:T(8,128)(2,1)S(1)} collective-permute-done((bf16[2,56,576]{2,1,0:T(8,128)(2,1)S(1)}, bf16[2,56,576]{2,1,0:T(8,128)(2,1)S(1)}, u32[]{:S(2)}, u32[]{:S(2)}) %collective-permute-start.58) | collective-permute-done | bytes 129056 | tf_op jit(solution)/shard_map/ppermute | solution.py:374
  (483 shorter events, 138.8 us)
Async XLA Ops:
  7.1 12.3 %collective-permute-start.3 = (bf16[256,768]{1,0:T(8,128)(2,1)S(1)}, bf16[256,768]{1,0:T(8,128)(2,1)S(1)}, u32[]{:S(2)}, u32[]{:S(2)}) collective-permute-start(bf16[256,768]{1,0:T(8,128)(2,1)S(1)} %bitcast.199), channel_id=1, source_target_pairs={{0,1},{1,0},{2,3},{3,2},{4,5},{5,4},{6,7},{7,6},{8,9},{9,8},{10,11... | collective-permute-start | bytes 1179656 | tf_op jit(solution)/shard_map/ppermute | solution.py:386
  9.8 9.9 %collective-permute-start.2 = (bf16[432,384]{1,0:T(8,128)(2,1)S(1)}, bf16[432,384]{1,0:T(8,128)(2,1)S(1)}, u32[]{:S(2)}, u32[]{:S(2)}) collective-permute-start(bf16[432,384]{1,0:T(8,128)(2,1)S(1)} %fusion.63), channel_id=1, source_target_pairs={{0,8},{2,10},{4,12},{6,14},{8,0},{10,2},{12,4},{14,6},{16,24},{18,... | collective-permute-start | bytes 995336 | tf_op jit(solution)/shard_map/ppermute | solution.py:374
  19.7 12.1 %collective-permute-start.6 = (bf16[256,768]{1,0:T(8,128)(2,1)S(1)}, bf16[256,768]{1,0:T(8,128)(2,1)S(1)}, u32[]{:S(2)}, u32[]{:S(2)}) collective-permute-start(bf16[256,768]{1,0:T(8,128)(2,1)S(1)} %get-tuple-element.139), channel_id=1, source_target_pairs={{0,4},{2,6},{4,0},{6,2},{8,12},{10,14},{12,8},{14,10},{16,20},{18,... | collective-permute-start | bytes 1179656 | tf_op jit(solution)/shard_map/ppermute | solution.py:374
  32.1 16.1 %collective-permute-start.9 = (bf16[432,384]{1,0:T(8,128)(2,1)S(1)}, bf16[432,384]{1,0:T(8,128)(2,1)S(1)}, u32[]{:S(2)}, u32[]{:S(2)}) collective-permute-start(bf16[432,384]{1,0:T(8,128)(2,1)S(1)} %fusion.63), channel_id=1, source_target_pairs={{0,16},{2,18},{4,20},{6,22},{8,24},{10,26},{12,28},{14,30},{16,0},... | collective-permute-start | bytes 995336 | tf_op jit(solution)/shard_map/ppermute | solution.py:374
  37.8 13.1 %collective-permute-start.8 = (bf16[4,2,56,576]{3,2,1,0:T(8,128)(2,1)S(1)}, bf16[4,2,56,576]{3,2,1,0:T(8,128)(2,1)S(1)}, u32[]{:S(2)}, u32[]{:S(2)}) collective-permute-start(bf16[4,2,56,576]{3,2,1,0:T(8,128)(2,1)S(1)} %pad_maximum_fusion.11.own_ref), channel_id=1, source_target_pairs={{0,2},{2,0},{4,6},{6,4},{8,10},{10,8},{12,14},{14,12},{16,18},{18,... | collective-permute-start | bytes 1548296 | tf_op jit(solution)/shard_map/ppermute | solution.py:374
  49.3 9.5 %collective-permute-start.11 = (bf16[256,768]{1,0:T(8,128)(2,1)S(1)}, bf16[256,768]{1,0:T(8,128)(2,1)S(1)}, u32[]{:S(2)}, u32[]{:S(2)}) collective-permute-start(bf16[256,768]{1,0:T(8,128)(2,1)S(1)} %get-tuple-element.147), channel_id=1, source_target_pairs={{0,4},{2,6},{4,0},{6,2},{8,12},{10,14},{12,8},{14,10},{16,20},{18,... | collective-permute-start | bytes 1179656 | tf_op jit(solution)/shard_map/ppermute | solution.py:374
  58.8 21.0 %collective-permute-start.13 = (bf16[384,512]{1,0:T(8,128)(2,1)S(1)}, bf16[384,512]{1,0:T(8,128)(2,1)S(1)}, u32[]{:S(2)}, u32[]{:S(2)}) collective-permute-start(bf16[384,512]{1,0:T(8,128)(2,1)S(1)} %fusion.9.refs_1_.refs_10_), channel_id=1, source_target_pairs={{0,16},{2,18},{4,20},{6,22},{8,24},{10,26},{12,28},{14,30},{16,0},... | collective-permute-start | bytes 1179656 | tf_op jit(solution)/shard_map/ppermute | solution.py:374
  61.6 18.4 %collective-permute-start.12 = (bf16[384,512]{1,0:T(8,128)(2,1)S(1)}, bf16[384,512]{1,0:T(8,128)(2,1)S(1)}, u32[]{:S(2)}, u32[]{:S(2)}) collective-permute-start(bf16[384,512]{1,0:T(8,128)(2,1)S(1)} %fusion.9.refs_1_.refs_10_), channel_id=1, source_target_pairs={{0,8},{2,10},{4,12},{6,14},{8,0},{10,2},{12,4},{14,6},{16,24},{18,... | collective-permute-start | bytes 1179656 | tf_op jit(solution)/shard_map/ppermute | solution.py:374
  63.0 16.9 %collective-permute-start.14 = (bf16[4,144,384]{2,1,0:T(8,128)(2,1)S(1)}, bf16[4,144,384]{2,1,0:T(8,128)(2,1)S(1)}, u32[]{:S(2)}, u32[]{:S(2)}) collective-permute-start(bf16[4,144,384]{2,1,0:T(8,128)(2,1)S(1)} %slice.420), channel_id=1, source_target_pairs={{0,4},{2,6},{4,0},{6,2},{8,12},{10,14},{12,8},{14,10},{16,20},{18,... | collective-permute-start | bytes 1327112 | tf_op jit(solution)/shard_map/ppermute | solution.py:374
  66.0 10.1 %collective-permute-start.15 = (bf16[4,96,384]{2,1,0:T(8,128)(2,1)S(1)}, bf16[4,96,384]{2,1,0:T(8,128)(2,1)S(1)}, u32[]{:S(2)}, u32[]{:S(2)}) collective-permute-start(bf16[4,96,384]{2,1,0:T(8,128)(2,1)S(1)} %get-tuple-element.285), channel_id=1, source_target_pairs={{0,1},{1,0},{2,3},{3,2},{4,5},{5,4},{6,7},{7,6},{8,9},{9,8},{10,11... | collective-permute-start | bytes 884744 | tf_op jit(solution)/shard_map/ppermute | solution.py:386
  80.0 12.2 %collective-permute-start.18 = (bf16[384,512]{1,0:T(8,128)(2,1)S(1)}, bf16[384,512]{1,0:T(8,128)(2,1)S(1)}, u32[]{:S(2)}, u32[]{:S(2)}) collective-permute-start(bf16[384,512]{1,0:T(8,128)(2,1)S(1)} %collective-permute-done.13.refs_1_.refs_6_), channel_id=1, source_target_pairs={{0,8},{2,10},{4,12},{6,14},{8,0},{10,2},{12,4},{14,6},{16,24},{18,... | collective-permute-start | bytes 1179656 | tf_op jit(solution)/shard_map/ppermute | solution.py:374
  81.9 22.0 %collective-permute-start.22 = (bf16[8,144,384]{2,1,0:T(8,128)(2,1)S(1)}, bf16[8,144,384]{2,1,0:T(8,128)(2,1)S(1)}, u32[]{:S(2)}, u32[]{:S(2)}) collective-permute-start(bf16[8,144,384]{2,1,0:T(8,128)(2,1)S(1)} %pad_maximum_fusion.3.one_own), channel_id=1, source_target_pairs={{0,1},{1,0},{2,3},{3,2},{4,5},{5,4},{6,7},{7,6},{8,9},{9,8},{10,11... | collective-permute-start | bytes 2654216 | tf_op jit(solution)/shard_map/ppermute | solution.py:386
  83.5 15.4 %collective-permute-start.23 = (bf16[2,4,96,384]{3,2,1,0:T(8,128)(2,1)S(1)}, bf16[2,4,96,384]{3,2,1,0:T(8,128)(2,1)S(1)}, u32[]{:S(2)}, u32[]{:S(2)}) collective-permute-start(bf16[2,4,96,384]{3,2,1,0:T(8,128)(2,1)S(1)} %pad_maximum_fusion.6.two_own), channel_id=1, source_target_pairs={{0,4},{2,6},{4,0},{6,2},{8,12},{10,14},{12,8},{14,10},{16,20},{18,... | collective-permute-start | bytes 1769480 | tf_op jit(solution)/shard_map/ppermute | solution.py:374
  114.8 10.0 %collective-permute-start.28 = (bf16[4,96,384]{2,1,0:T(8,128)(2,1)}, bf16[4,96,384]{2,1,0:T(8,128)(2,1)S(1)}, u32[]{:S(2)}, u32[]{:S(2)}) collective-permute-start(bf16[4,96,384]{2,1,0:T(8,128)(2,1)} %get-tuple-element.182), channel_id=1, source_target_pairs={{0,4},{2,6},{4,0},{6,2},{8,12},{10,14},{12,8},{14,10},{16,20},{18,... | collective-permute-start | bytes 884744 | tf_op jit(solution)/shard_map/ppermute | solution.py:374
  124.9 15.5 %collective-permute-start.30 = (bf16[8,96,384]{2,1,0:T(8,128)(2,1)S(1)}, bf16[8,96,384]{2,1,0:T(8,128)(2,1)S(1)}, u32[]{:S(2)}, u32[]{:S(2)}) collective-permute-start(bf16[8,96,384]{2,1,0:T(8,128)(2,1)S(1)} %constant_dynamic-update-slice_fusion.4.one_own), channel_id=1, source_target_pairs={{0,1},{1,0},{2,3},{3,2},{4,5},{5,4},{6,7},{7,6},{8,9},{9,8},{10,11... | collective-permute-start | bytes 1769480 | tf_op jit(solution)/shard_map/ppermute | solution.py:386
  127.2 14.9 %collective-permute-start.31 = (bf16[2,4,96,384]{3,2,1,0:T(8,128)(2,1)S(1)}, bf16[2,4,96,384]{3,2,1,0:T(8,128)(2,1)S(1)}, u32[]{:S(2)}, u32[]{:S(2)}) collective-permute-start(bf16[2,4,96,384]{3,2,1,0:T(8,128)(2,1)S(1)} %pad_maximum_fusion.7.two_own), channel_id=1, source_target_pairs={{0,4},{2,6},{4,0},{6,2},{8,12},{10,14},{12,8},{14,10},{16,20},{18,... | collective-permute-start | bytes 1769480 | tf_op jit(solution)/shard_map/ppermute | solution.py:374
  164.8 13.5 %collective-permute-start.35 = (bf16[4,2,48,768]{3,2,0,1:T(8,128)(2,1)S(1)}, bf16[4,2,48,768]{3,2,0,1:T(8,128)(2,1)S(1)}, u32[]{:S(2)}, u32[]{:S(2)}) collective-permute-start(bf16[4,2,48,768]{3,2,0,1:T(8,128)(2,1)S(1)} %select_bitcast_fusion.2), channel_id=1, source_target_pairs={{0,2},{2,0},{4,6},{6,4},{8,10},{10,8},{12,14},{14,12},{16,18},{18,... | collective-permute-start | bytes 1769480 | tf_op jit(solution)/shard_map/ppermute | solution.py:374
  180.8 32.9 %collective-permute-start.42 = (bf16[4,2,240,384]{3,2,0,1:T(8,128)(2,1)}, bf16[4,2,240,384]{3,2,0,1:T(8,128)(2,1)}, u32[]{:S(2)}, u32[]{:S(2)}) collective-permute-start(bf16[4,2,240,384]{3,2,0,1:T(8,128)(2,1)} %pad_maximum_fusion), channel_id=1, source_target_pairs={{0,1},{1,0},{2,3},{3,2},{4,5},{5,4},{6,7},{7,6},{8,9},{9,8},{10,11... | collective-permute-start | bytes 4423688 | tf_op jit(solution)/shard_map/ppermute | solution.py:386
  181.4 31.6 %collective-permute-start.43 = (bf16[4,192,768]{2,1,0:T(8,128)(2,1)}, bf16[4,192,768]{2,1,0:T(8,128)(2,1)}, u32[]{:S(2)}, u32[]{:S(2)}) collective-permute-start(bf16[4,192,768]{2,1,0:T(8,128)(2,1)} %select_bitcast_fusion), channel_id=1, source_target_pairs={{0,4},{2,6},{4,0},{6,2},{8,12},{10,14},{12,8},{14,10},{16,20},{18,... | collective-permute-start | bytes 3538952 | tf_op jit(solution)/shard_map/ppermute | solution.py:374
  216.6 10.8 %collective-permute-start.44 = (bf16[384,512]{1,0:T(8,128)(2,1)S(1)}, bf16[384,512]{1,0:T(8,128)(2,1)S(1)}, u32[]{:S(2)}, u32[]{:S(2)}) collective-permute-start(bf16[384,512]{1,0:T(8,128)(2,1)S(1)} %add_convert_fusion.8), channel_id=1, source_target_pairs={{0,8},{2,10},{4,12},{6,14},{8,0},{10,2},{12,4},{14,6},{16,24},{18,... | collective-permute-start | bytes 1179656 | tf_op jit(solution)/shard_map/ppermute | solution.py:374
  219.3 14.8 %collective-permute-start.48 = (bf16[4,192,384]{2,1,0:T(8,128)(2,1)S(1)}, bf16[4,192,384]{2,1,0:T(8,128)(2,1)S(1)}, u32[]{:S(2)}, u32[]{:S(2)}) collective-permute-start(bf16[4,192,384]{2,1,0:T(8,128)(2,1)S(1)} %broadcast_select_fusion), channel_id=1, source_target_pairs={{0,1},{1,0},{2,3},{3,2},{4,5},{5,4},{6,7},{7,6},{8,9},{9,8},{10,11... | collective-permute-start | bytes 1769480 | tf_op jit(solution)/shard_map/ppermute | solution.py:386
  220.3 18.0 %collective-permute-start.47 = (bf16[4,240,384]{2,1,0:T(8,128)(2,1)S(1)}, bf16[4,240,384]{2,1,0:T(8,128)(2,1)S(1)}, u32[]{:S(2)}, u32[]{:S(2)}) collective-permute-start(bf16[4,240,384]{2,1,0:T(8,128)(2,1)S(1)} %select_bitcast_fusion.1), channel_id=1, source_target_pairs={{0,4},{2,6},{4,0},{6,2},{8,12},{10,14},{12,8},{14,10},{16,20},{18,... | collective-permute-start | bytes 2211848 | tf_op jit(solution)/shard_map/ppermute | solution.py:374
  227.5 18.2 %collective-permute-start.46 = (bf16[384,512]{1,0:T(8,128)(2,1)S(1)}, bf16[384,512]{1,0:T(8,128)(2,1)S(1)}, u32[]{:S(2)}, u32[]{:S(2)}) collective-permute-start(bf16[384,512]{1,0:T(8,128)(2,1)S(1)} %add_convert_fusion.9), channel_id=1, source_target_pairs={{0,8},{2,10},{4,12},{6,14},{8,0},{10,2},{12,4},{14,6},{16,24},{18,... | collective-permute-start | bytes 1179656 | tf_op jit(solution)/shard_map/ppermute | solution.py:374
  233.8 20.0 %collective-permute-start.45 = (bf16[384,512]{1,0:T(8,128)(2,1)S(1)}, bf16[384,512]{1,0:T(8,128)(2,1)S(1)}, u32[]{:S(2)}, u32[]{:S(2)}) collective-permute-start(bf16[384,512]{1,0:T(8,128)(2,1)S(1)} %add_convert_fusion.7), channel_id=1, source_target_pairs={{0,16},{2,18},{4,20},{6,22},{8,24},{10,26},{12,28},{14,30},{16,0},... | collective-permute-start | bytes 1179656 | tf_op jit(solution)/shard_map/ppermute | solution.py:374
  241.5 17.8 %collective-permute-start.52 = (bf16[256,768]{1,0:T(8,128)(2,1)S(1)}, bf16[256,768]{1,0:T(8,128)(2,1)S(1)}, u32[]{:S(2)}, u32[]{:S(2)}) collective-permute-start(bf16[256,768]{1,0:T(8,128)(2,1)S(1)} %slice.661), channel_id=1, source_target_pairs={{0,4},{2,6},{4,0},{6,2},{8,12},{10,14},{12,8},{14,10},{16,20},{18,... | collective-permute-start | bytes 1179656 | tf_op jit(solution)/shard_map/ppermute | solution.py:374
  244.0 15.2 %collective-permute-start.49 = (bf16[432,384]{1,0:T(8,128)(2,1)S(1)}, bf16[432,384]{1,0:T(8,128)(2,1)S(1)}, u32[]{:S(2)}, u32[]{:S(2)}) collective-permute-start(bf16[432,384]{1,0:T(8,128)(2,1)S(1)} %get-tuple-element.281), channel_id=1, source_target_pairs={{0,8},{2,10},{4,12},{6,14},{8,0},{10,2},{12,4},{14,6},{16,24},{18,... | collective-permute-start | bytes 995336 | tf_op jit(solution)/shard_map/ppermute | solution.py:374
  267.3 11.5 %collective-permute-start.53 = (bf16[256,768]{1,0:T(8,128)(2,1)S(1)}, bf16[256,768]{1,0:T(8,128)(2,1)S(1)}, u32[]{:S(2)}, u32[]{:S(2)}) collective-permute-start(bf16[256,768]{1,0:T(8,128)(2,1)S(1)} %slice.660), channel_id=1, source_target_pairs={{0,4},{2,6},{4,0},{6,2},{8,12},{10,14},{12,8},{14,10},{16,20},{18,... | collective-permute-start | bytes 1179656 | tf_op jit(solution)/shard_map/ppermute | solution.py:374
  268.5 26.1 %collective-permute-start.56 = (bf16[432,384]{1,0:T(8,128)(2,1)S(1)}, bf16[432,384]{1,0:T(8,128)(2,1)S(1)}, u32[]{:S(2)}, u32[]{:S(2)}) collective-permute-start(bf16[432,384]{1,0:T(8,128)(2,1)S(1)} %add_convert_fusion.13), channel_id=1, source_target_pairs={{0,16},{2,18},{4,20},{6,22},{8,24},{10,26},{12,28},{14,30},{16,0},... | collective-permute-start | bytes 995336 | tf_op jit(solution)/shard_map/ppermute | solution.py:374
  268.6 26.0 %collective-permute-start.55 = (bf16[432,384]{1,0:T(8,128)(2,1)S(1)}, bf16[432,384]{1,0:T(8,128)(2,1)S(1)}, u32[]{:S(2)}, u32[]{:S(2)}) collective-permute-start(bf16[432,384]{1,0:T(8,128)(2,1)S(1)} %copy-done.85), channel_id=1, source_target_pairs={{0,8},{2,10},{4,12},{6,14},{8,0},{10,2},{12,4},{14,6},{16,24},{18,... | collective-permute-start | bytes 995336 | tf_op jit(solution)/shard_map/ppermute | solution.py:374
  270.6 23.9 %collective-permute-start.58 = (bf16[2,56,576]{2,1,0:T(8,128)(2,1)S(1)}, bf16[2,56,576]{2,1,0:T(8,128)(2,1)S(1)}, u32[]{:S(2)}, u32[]{:S(2)}) collective-permute-start(bf16[2,56,576]{2,1,0:T(8,128)(2,1)S(1)} %get-tuple-element.305), channel_id=1, source_target_pairs={{0,8},{2,10},{4,12},{6,14},{8,0},{10,2},{12,4},{14,6},{16,24},{18,... | collective-permute-start | bytes 387080 | tf_op jit(solution)/shard_map/ppermute | solution.py:374
  276.2 18.3 %collective-permute-start.60 = (bf16[2,56,576]{2,1,0:T(8,128)(2,1)S(1)}, bf16[2,56,576]{2,1,0:T(8,128)(2,1)S(1)}, u32[]{:S(2)}, u32[]{:S(2)}) collective-permute-start(bf16[2,56,576]{2,1,0:T(8,128)(2,1)S(1)} %fusion.64), channel_id=1, source_target_pairs={{0,16},{2,18},{4,20},{6,22},{8,24},{10,26},{12,28},{14,30},{16,0},... | collective-permute-start | bytes 387080 | tf_op jit(solution)/shard_map/ppermute | solution.py:374
  279.0 18.7 %collective-permute-start.54 = (bf16[256,768]{1,0:T(8,128)(2,1)S(1)}, bf16[256,768]{1,0:T(8,128)(2,1)S(1)}, u32[]{:S(2)}, u32[]{:S(2)}) collective-permute-start(bf16[256,768]{1,0:T(8,128)(2,1)S(1)} %select_convert_fusion), channel_id=1, source_target_pairs={{0,1},{1,0},{2,3},{3,2},{4,5},{5,4},{6,7},{7,6},{8,9},{9,8},{10,11... | collective-permute-start | bytes 1179656 | tf_op jit(solution)/shard_map/ppermute | solution.py:386
  (141 other events, 807.5 us)
